TPU v7x, 32 devices: a whole 2x2x4 slice. The times are simulated.
32 devices in a mesh: row: 8 (over y, x, core), col: 4 (over z).
Axes of the slice: x: 2, y: 2, z: 4, core: 2. Of those that a mesh axis runs over, the one named last changes fastest.
Arguments:
- matrix: float32 [16384, 16384], P('row', 'col'), may hold values from -80 to 80
Outputs:
- reduced: float32 [16384, 16384], P('row', 'col')
All inputs are finite; a program needn't handle non-finite values.
Results may differ from a plain program's by a relative error of at most 0.0003.
Values sent between devices are 32-bit elements; how exact they have to be, the bound alone decides.
A program may use at most 128 MiB of HBM per device.

v0:
```python
import jax
import jax.numpy as jnp
from jax import lax
from jax.experimental import pallas as pl
from jax.experimental.pallas import tpu as pltpu
from jax.sharding import PartitionSpec as P

B = 64


highest = lax.Precision.HIGHEST
MESH = pl.DeviceIdType.MESH
f32 = jnp.float32
bf16 = jnp.bfloat16


def product(left, right):
    return jnp.dot(left, right, precision=highest, preferred_element_type=f32)


def split(x):
    upper = x.astype(bf16)
    return upper, (x - upper.astype(f32)).astype(bf16)


def product_nt(left, right):
    return lax.dot_general(
        left, right, (((1,), (1,)), ((), ())), precision=highest, preferred_element_type=f32
    )


def factor_values(gram, top):
    rows = lax.broadcasted_iota(jnp.int32, (B, 2 * B), 0)
    lanes = lax.broadcasted_iota(jnp.int32, (B, 2 * B), 1)
    eye = jnp.where(rows + B == lanes, f32(1.0), f32(0.0))
    small_rows = lax.broadcasted_iota(jnp.int32, (B, B), 0)
    small_lanes = lax.broadcasted_iota(jnp.int32, (B, B), 1)
    eye_half = jnp.where(small_rows == small_lanes, f32(1.0), f32(0.0))
    work = jnp.concatenate([gram, eye_half], axis=1)
    for j in range(B):
        inverse = 1.0 / jnp.sqrt(work[j : j + 1, j : j + 1])
        row = work[j : j + 1, :] * inverse
        column = work[:, j : j + 1] * inverse
        lowered = work - column * row
        work = jnp.where(rows > j, lowered, jnp.where(rows == j, row, work))
    lower_inverse = work[:, B:]
    top_basis = product_nt(top, lower_inverse)
    top_turned = product_nt(lower_inverse, top)
    q = jnp.concatenate([top_basis, eye_half], axis=1)
    t = jnp.concatenate([top_turned, eye_half], axis=1)
    signs = jnp.zeros((1, B), f32)
    sign_lane = lax.broadcasted_iota(jnp.int32, (1, B), 1)
    reciprocals = jnp.zeros((B, 1), f32)
    sublane = lax.broadcasted_iota(jnp.int32, (B, 1), 0)
    one_row = lax.broadcasted_iota(jnp.int32, (1, 2 * B), 1)
    for j in range(B):
        pivot = q[j : j + 1, j : j + 1]
        sign = jnp.where(pivot >= 0, f32(-1.0), f32(1.0))
        inverse = 1.0 / (pivot - sign)
        row_q = q[j : j + 1, :] - jnp.where(one_row == j, sign, f32(0.0))
        row_t = t[j : j + 1, :] - jnp.where(one_row == j, sign, f32(0.0))
        below_q = q[:, j : j + 1] * inverse
        below_t = t[:, j : j + 1] * inverse
        q = jnp.where(rows > j, q - below_q * row_q, jnp.where(rows == j, row_q, q))
        t = jnp.where(rows > j, t - below_t * row_t, t)
        signs = jnp.where(sign_lane == j, sign, signs)
        reciprocals = jnp.where(sublane == j, inverse, reciprocals)
    upper = jnp.where(small_lanes >= small_rows, q[:, :B], f32(0.0))
    unit_inverse = q[:, B:]
    upper_inverse_turned = t[:, B:] * reciprocals
    factor = -product_nt(upper * signs, unit_inverse)
    factor_turned = -product_nt(unit_inverse, upper * signs)
    first = product(upper_inverse_turned, lower_inverse)
    second = upper_inverse_turned * signs
    return first, second, factor, factor_turned


def remote(src, dst, send_sem, recv_sem, device):
    return pltpu.make_async_remote_copy(
        src_ref=src,
        dst_ref=dst,
        send_sem=send_sem,
        recv_sem=recv_sem,
        device_id=device,
        device_id_type=MESH,
    )


def greet_all(height, breadth, me_row, me_col):
    count = height * breadth
    me = me_row * breadth + me_col
    barrier = pltpu.get_barrier_semaphore()

    def signal(step, carry):
        other = lax.rem(me + step, count)
        pl.semaphore_signal(
            barrier,
            inc=1,
            device_id=(other // breadth, lax.rem(other, breadth)),
            device_id_type=MESH,
        )
        return carry

    lax.fori_loop(1, count, signal, 0)
    pl.semaphore_wait(barrier, count - 1)


def gather_axis(buffer, mine, count, target, send_sems, recv_sems, skip=None):
    for step in range(1, count):
        other = lax.rem(mine + step, count)
        copy = remote(
            buffer.at[mine], buffer.at[mine], send_sems.at[step], recv_sems.at[mine], target(other)
        )
        if skip is None:
            copy.start()
        else:
            pl.when(other != skip)(copy.start)


def gather_sent(buffer, mine, count, target, send_sems, recv_sems, skip=None):
    for step in range(1, count):
        other = lax.rem(mine + step, count)
        copy = remote(
            buffer.at[mine], buffer.at[mine], send_sems.at[step], recv_sems.at[mine], target(other)
        )
        if skip is None:
            copy.wait_send()
        else:
            pl.when(other != skip)(copy.wait_send)


def gather_received(buffer, mine, count, target, send_sems, recv_sems):
    for step in range(1, count):
        other = lax.rem(mine + step, count)
        remote(
            buffer.at[other], buffer.at[other], send_sems.at[step], recv_sems.at[other], target(other)
        ).wait_recv()


def pair_copies(buffer, mine, count, target, send_sems, recv_sems, skip):
    partner = mine + 1 - 2 * lax.rem(mine, 2)

    def copy(slot, step, other):
        made = remote(
            buffer.at[slot], buffer.at[slot], send_sems.at[step], recv_sems.at[slot], target(other)
        )
        return other != skip, made

    direct = []
    passed = []
    for step in range(2, count, 2):
        other = lax.rem(mine + step, count)
        direct.append(copy(mine, step, other))
        passed.append((other, copy(other, step + 1, partner)))
    direct.append(copy(mine, 1, partner))
    return partner, direct, passed


def pair_gather(buffer, mine, count, target, send_sems, recv_sems, skip=-1):
    partner, direct, passed = pair_copies(buffer, mine, count, target, send_sems, recv_sems, skip)

    def received(slot):
        remote(
            buffer.at[slot], buffer.at[slot], send_sems.at[0], recv_sems.at[slot], target(partner)
        ).wait_recv()

    for allowed, copy in direct:
        pl.when(allowed)(copy.start)
    for slot, (allowed, copy) in passed:
        received(slot)
        pl.when(allowed)(copy.start)
    received(partner)
    for step in range(2, count, 2):
        received(lax.rem(partner + step, count))


def pair_sent(buffer, mine, count, target, send_sems, recv_sems, skip=-1):
    _, direct, passed = pair_copies(buffer, mine, count, target, send_sems, recv_sems, skip)
    for allowed, copy in direct + [entry for _, entry in passed]:
        pl.when(allowed)(copy.wait_send)


def spread_kernel(
    height, breadth, own, pc, pr, stats, ex,
    local_sem, scatter_sems, role_sems, role_local, plane_sems, pc_sems, line_sems, pr_sems,
    ex_sends, ex_recvs,
):
    me_row, me_col = lax.axis_index("row"), lax.axis_index("col")
    width = own.shape[2]
    next_row = lax.rem(me_row + 1, height)
    in_plane = lambda other: (other, me_col)
    in_line = lambda other: (me_row, other)
    root = me_row == 0
    chunk = me_row * breadth + me_col
    local_role = jnp.logical_and(root, chunk // height == me_col)

    greet_all(height, breadth, me_row, me_col)

    def scatter_copy(i):
        return remote(own.at[i], pc.at[i], scatter_sems.at[i], pc_sems.at[i], (i, me_col))

    def role_copy(i):
        g = me_col * height + i
        k = lax.rem(g, breadth)
        r = g // breadth
        itself = jnp.logical_and(r == 0, k == me_col)
        return itself, remote(own.at[i], pr.at[k], role_sems.at[i], pr_sems.at[k], (r, k)), k

    def first_copies():
        made = [
            remote(own.at[0], pc.at[0], plane_sems.at[j], pc_sems.at[0], (j, me_col))
            for j in [1] + list(range(2, height, 2))
        ]
        return made + [
            remote(own.at[m], pc.at[m], plane_sems.at[m + 1], pc_sems.at[m], (1, me_col))
            for m in range(2, height, 2)
        ]

    @pl.when(root)
    def _():
        for i in range(1, height):
            scatter_copy(i).start()
        for i in range(height):
            itself, copy, k = role_copy(i)
            pl.when(jnp.logical_not(itself))(copy.start)
            local = pltpu.make_async_copy(own.at[i], pr.at[k], role_local)
            pl.when(itself)(local.start)
        for copy in first_copies():
            copy.start()
        whole = pltpu.make_async_copy(own, pc, local_sem)
        whole.start()
        whole.wait()

    @pl.when(local_role)
    def _():
        pltpu.make_async_copy(own.at[0], pr.at[me_col], role_local).wait()

    @pl.when(jnp.logical_not(root))
    def _():
        remote(
            pc.at[me_row], pc.at[me_row], plane_sems.at[0], pc_sems.at[me_row], (next_row, me_col)
        ).wait_recv()

    @pl.when(jnp.logical_not(local_role))
    def _():
        remote(
            pr.at[me_col], pr.at[me_col], line_sems.at[0], pr_sems.at[me_col], (next_row, me_col)
        ).wait_recv()

    gather_axis(pr, me_col, breadth, in_line, line_sems, pr_sems)

    @pl.when(jnp.logical_not(root))
    def _():
        pair_gather(pc, me_row, height, in_plane, plane_sems, pc_sems, skip=0)

    gram = jnp.zeros((B, B), f32)
    top = jnp.zeros((B, B), f32)
    positions = lax.broadcasted_iota(jnp.int32, (width, B), 0)
    slots = lax.broadcasted_iota(jnp.int32, (width, B), 1)
    for i in range(height):
        piece = pc[i]
        start = (me_col * height + i) * width - B
        gram = gram + product_nt(piece, piece)
        onehot = jnp.where(positions + start == slots, f32(1.0), f32(0.0))
        top = top + product(piece, onehot)
    ex[me_col] = jnp.concatenate([gram, top], axis=1)
    gather_axis(ex, me_col, breadth, in_line, ex_sends, ex_recvs)
    gather_received(ex, me_col, breadth, in_line, ex_sends, ex_recvs)
    total = ex[0]
    for k in range(1, breadth):
        total = total + ex[k]
    stats[...] = total
    gather_received(pr, me_col, breadth, in_line, line_sems, pr_sems)
    gather_sent(ex, me_col, breadth, in_line, ex_sends, ex_recvs)
    gather_sent(pr, me_col, breadth, in_line, line_sems, pr_sems)

    @pl.when(root)
    def _():
        for i in range(1, height):
            scatter_copy(i).wait_send()
        for i in range(height):
            itself, copy, _ = role_copy(i)
            pl.when(jnp.logical_not(itself))(copy.wait_send)
        for copy in first_copies():
            copy.wait_send()

    @pl.when(jnp.logical_not(root))
    def _():
        pair_sent(pc, me_row, height, in_plane, plane_sems, pc_sems, skip=0)


def spread(own, height, breadth):
    width = own.shape[2]
    vmem = pl.BlockSpec(memory_space=pltpu.VMEM)
    dma = pltpu.SemaphoreType.DMA
    return pl.pallas_call(
        lambda *refs: spread_kernel(height, breadth, *refs),
        out_shape=[
            jax.ShapeDtypeStruct((height, B, width), f32),
            jax.ShapeDtypeStruct((breadth, B, width), f32),
            jax.ShapeDtypeStruct((B, 2 * B), f32),
        ],
        in_specs=[vmem],
        out_specs=[vmem] * 3,
        scratch_shapes=[
            pltpu.VMEM((breadth, B, 2 * B), f32),
            dma(()),
            dma((height,)),
            dma((height,)),
            dma(()),
            dma((height,)),
            dma((height,)),
            dma((breadth,)),
            dma((breadth,)),
            dma((breadth,)),
            dma((breadth,)),
        ],
        compiler_params=pltpu.CompilerParams(collective_id=0, has_side_effects=True),
        name="spread",
    )(own)


def vectors_kernel(height, breadth, stats, pc, pr, vc, vr, factor_ref, turned_ref, halves):
    first, second, factor, turned = factor_values(stats[:, :B], stats[:, B:].T)
    factor_ref[...] = factor
    turned_ref[...] = turned
    width = pc.shape[2]
    slots = lax.broadcasted_iota(jnp.int32, (B, width), 0)
    positions = lax.broadcasted_iota(jnp.int32, (B, width), 1)
    for pieces, out, base, count in (
        (pc, vc, lax.axis_index("col") * height, height),
        (pr, vr, lax.axis_index("row") * breadth, breadth),
    ):
        for i in range(count):
            start = (base + i) * width - B
            onehot = jnp.where(positions + start == slots, f32(1.0), f32(0.0))
            out[:, i * width : (i + 1) * width] = product(first, pieces[i]) - product(
                second, onehot
            )
    upper, lower = split(vc[...])
    halves[:B, :] = upper
    halves[B:, :] = lower


def vectors_of(stats, pc, pr, height, breadth):
    width = pc.shape[2]
    vmem = pl.BlockSpec(memory_space=pltpu.VMEM)
    return pl.pallas_call(
        lambda *refs: vectors_kernel(height, breadth, *refs),
        out_shape=[
            jax.ShapeDtypeStruct((B, height * width), f32),
            jax.ShapeDtypeStruct((B, breadth * width), f32),
            jax.ShapeDtypeStruct((B, B), f32),
            jax.ShapeDtypeStruct((B, B), f32),
            jax.ShapeDtypeStruct((2 * B, height * width), bf16),
        ],
        in_specs=[vmem] * 3,
        out_specs=[vmem] * 5,
        name="vectors",
    )(stats, pc, pr)


def image_kernel(
    height, breadth, z, vc, wc, wr, projected, rs, ex,
    rs_sends, rs_recvs, line_sems, wr_sems, role_sem, plane_sems, wc_sems, ex_sends, ex_recvs,
):
    me_row, me_col = lax.axis_index("row"), lax.axis_index("col")
    width = z.shape[2]
    in_plane = lambda other: (other, me_col)
    in_line = lambda other: (me_row, other)
    chunk = me_row * breadth + me_col
    to_row = lax.rem(chunk, height)
    to_col = chunk // height
    itself = jnp.logical_and(to_row == me_row, to_col == me_col)

    greet_all(height, breadth, me_row, me_col)

    def part_copy(step):
        other = lax.rem(me_col + step, breadth)
        return remote(
            z.at[other], rs.at[me_col], rs_sends.at[step], rs_recvs.at[me_col], in_line(other)
        )

    for step in range(1, breadth):
        part_copy(step).start()
    rs[me_col] = z[me_col]
    gather_received(rs, me_col, breadth, in_line, rs_sends, rs_recvs)
    total = rs[0]
    for k in range(1, breadth):
        total = total + rs[k]
    wr[me_col] = total
    role = remote(wr.at[me_col], wc.at[to_row], role_sem, wc_sems.at[to_row], (to_row, to_col))

    @pl.when(jnp.logical_not(itself))
    def _():
        role.start()

    gather_axis(wr, me_col, breadth, in_line, line_sems, wr_sems)

    @pl.when(itself)
    def _():
        wc[me_row] = total

    @pl.when(jnp.logical_not(itself))
    def _():
        remote(
            wc.at[me_row], wc.at[me_row], plane_sems.at[0], wc_sems.at[me_row],
            (lax.rem(me_row + 1, height), me_col),
        ).wait_recv()

    pair_gather(wc, me_row, height, in_plane, plane_sems, wc_sems)
    partial = jnp.zeros((B, B), f32)
    for i in range(height):
        partial = partial + product_nt(wc[i], vc[:, i * width : (i + 1) * width])
    ex[me_col] = jnp.concatenate([partial, jnp.zeros((B, B), f32)], axis=1)
    gather_axis(ex, me_col, breadth, in_line, ex_sends, ex_recvs)
    gather_received(ex, me_col, breadth, in_line, ex_sends, ex_recvs)
    summed = ex[0]
    for k in range(1, breadth):
        summed = summed + ex[k]
    projected[...] = summed
    gather_received(wr, me_col, breadth, in_line, line_sems, wr_sems)
    for step in range(1, breadth):
        part_copy(step).wait_send()

    @pl.when(jnp.logical_not(itself))
    def _():
        role.wait_send()

    gather_sent(wr, me_col, breadth, in_line, line_sems, wr_sems)
    pair_sent(wc, me_row, height, in_plane, plane_sems, wc_sems)
    gather_sent(ex, me_col, breadth, in_line, ex_sends, ex_recvs)


def images(z, vc, height, breadth):
    width = z.shape[2]
    vmem = pl.BlockSpec(memory_space=pltpu.VMEM)
    dma = pltpu.SemaphoreType.DMA
    return pl.pallas_call(
        lambda *refs: image_kernel(height, breadth, *refs),
        out_shape=[
            jax.ShapeDtypeStruct((height, B, width), f32),
            jax.ShapeDtypeStruct((breadth, B, width), f32),
            jax.ShapeDtypeStruct((B, 2 * B), f32),
        ],
        in_specs=[vmem] * 2,
        out_specs=[vmem] * 3,
        scratch_shapes=[
            pltpu.VMEM((breadth, B, width), f32),
            pltpu.VMEM((breadth, B, 2 * B), f32),
            dma((breadth,)),
            dma((breadth,)),
            dma((breadth,)),
            dma((breadth,)),
            dma(()),
            dma((height,)),
            dma((height,)),
            dma((breadth,)),
            dma((breadth,)),
        ],
        compiler_params=pltpu.CompilerParams(collective_id=1, has_side_effects=True),
        name="images",
    )(z, vc)


def image_part_kernel(block, halves, out):
    nt = (((1,), (1,)), ((), ()))
    rows, cols = block.shape
    size = min(512, cols)
    both = jnp.zeros((rows, 2 * B), f32)
    for start in range(0, cols, size):
        part = slice(start, start + size)
        upper, lower = split(block[:, part])
        both = both + lax.dot_general(upper, halves[:, part], nt, preferred_element_type=f32)
        low = lax.dot_general(lower, halves[:, part], nt, preferred_element_type=f32)
        both = both + jnp.where(lax.broadcasted_iota(jnp.int32, both.shape, 1) < B, low, f32(0.0))
    turned = both.T
    out[0] = turned[:B, :] + turned[B:, :]


def image_part(matrix, halves, width):
    rows, cols = matrix.shape
    return pl.pallas_call(
        image_part_kernel,
        grid=(rows // width,),
        out_shape=jax.ShapeDtypeStruct((rows // width, B, width), f32),
        in_specs=[
            pl.BlockSpec((width, cols), lambda i: (i, 0)),
            pl.BlockSpec((2 * B, cols), lambda i: (0, 0)),
        ],
        out_specs=pl.BlockSpec((1, B, width), lambda i: (i, 0, 0)),
        name="image_part",
    )(matrix, halves)


def final_kernel(block, left, right, out):
    cols = block.shape[1]
    size = min(512, cols)
    for start in range(0, cols, size):
        part = slice(start, start + size)
        out[:, part] = block[:, part] - jnp.dot(
            left[...], right[:, part], preferred_element_type=f32
        )


def final(matrix, left, right):
    rows, cols = matrix.shape
    tile = min(512, rows)
    depth = left.shape[1]
    return pl.pallas_call(
        final_kernel,
        grid=(rows // tile,),
        out_shape=jax.ShapeDtypeStruct((rows, cols), f32),
        in_specs=[
            pl.BlockSpec((tile, cols), lambda i: (i, 0)),
            pl.BlockSpec((tile, depth), lambda i: (i, 0)),
            pl.BlockSpec((depth, cols), lambda i: (0, 0)),
        ],
        out_specs=pl.BlockSpec((tile, cols), lambda i: (i, 0)),
        name="final",
    )(matrix, left, right)


def updates_kernel(height, breadth, projected, factor, turned, vc, vr, wc, wr, left, right):
    inner = product(turned[...], product(projected[:, :B], factor[...]))
    mix = jnp.concatenate([turned[...], -0.5 * inner], axis=1)
    width = wc.shape[2]
    for i in range(height):
        part = slice(i * width, (i + 1) * width)
        v = vc[:, part]
        u = product(mix, jnp.concatenate([wc[i], v], axis=0))
        upper, lower = split(jnp.concatenate([u, v], axis=0))
        right[: 2 * B, part] = upper
        right[2 * B : 4 * B, part] = upper
        right[4 * B :, part] = lower
    for i in range(breadth):
        part = slice(i * width, (i + 1) * width)
        v = vr[:, part]
        u = product(mix, jnp.concatenate([wr[i], v], axis=0))
        upper, lower = split(jnp.concatenate([v, u], axis=0).T)
        left[part, : 2 * B] = upper
        left[part, 2 * B : 4 * B] = lower
        left[part, 4 * B :] = upper


def updates(projected, factor, turned, vc, vr, wc, wr):
    height, breadth = wc.shape[0], wr.shape[0]
    vmem = pl.BlockSpec(memory_space=pltpu.VMEM)
    return pl.pallas_call(
        lambda *refs: updates_kernel(height, breadth, *refs),
        out_shape=[
            jax.ShapeDtypeStruct((vr.shape[1], 6 * B), bf16),
            jax.ShapeDtypeStruct((6 * B, vc.shape[1]), bf16),
        ],
        in_specs=[vmem] * 7,
        out_specs=[vmem] * 2,
        name="updates",
    )(projected, factor, turned, vc, vr, wc, wr)


def shards(height, breadth, matrix):
    rows, cols = matrix.shape
    width = cols // height
    global_cols = lax.axis_index("col") * cols + jnp.arange(cols, dtype=jnp.int32)
    masked = jnp.where(global_cols[None, :] >= B, matrix[0:B, :], f32(0.0))
    own = masked.reshape(B, height, width).transpose(1, 0, 2)
    pc, pr, stats = spread(own, height, breadth)
    vc, vr, factor, turned, halves = vectors_of(stats, pc, pr, height, breadth)
    z = image_part(matrix, halves, width)
    wc, wr, projected = images(z, vc, height, breadth)
    left, right = updates(projected, factor, turned, vc, vr, wc, wr)
    return final(matrix, left, right)


def solution(mesh):
    placed = (P("row", "col"),)
    height, breadth = mesh.shape["row"], mesh.shape["col"]
    return jax.shard_map(
        lambda matrix: shards(height, breadth, matrix),
        mesh=mesh,
        in_specs=placed,
        out_specs=P("row", "col"),
        check_vma=False,
    )
```

profile of v0, /device:TPU:4, one launch (start us, length us, event | category | flops | bytes accessed | tf_op | source)
XLA Modules:
  0.0 143.9 jit_solution(10750623498559632982)
XLA Ops:
  0.0 1.3 slice_select_fusion
  1.3 1.1 copy.5
  2.4 35.6 %spread.1 = (f32[8,64,512]{2,1,0:T(8,128)}, f32[4,64,512]{2,1,0:T(8,128)}, f32[64,128]{1,0:T(8,128)}) custom-call(f32[8,64,512]{2,1,0:T(8,128)} %bitcast.7), custom_call_target="tpu_custom_call" | custom-call | tf_op jit(solution)/shard_map/spread/pallas_call | solution.py:296
  38.0 17.6 %vectors.1 = (f32[64,4096]{1,0:T(8,128)}, f32[64,2048]{1,0:T(8,128)}, f32[64,64]{1,0:T(8,128)}, f32[64,64]{1,0:T(8,128)}, bf16[128,4096]{1,0:T(8,128)(2,1)}) custom-call(f32[64,128]{1,0:T(8,128)} %get-tuple-element.18.refs_0_, f32[8,64,512]{2,1,0:T(8,128)} %get-tuple-element.19.refs_1_, f32[4,64,512]{2,1,0:T(8,128)} %get-tuple-element.20.refs_2_), custom_call_target="tpu_custom_call" | custom-call | tf_op jit(solution)/shard_map/vectors/pallas_call | solution.py:348
  55.6 15.3 %image_part.1.refs_0_ = f32[4,64,512]{2,1,0:T(8,128)} custom-call(f32[2048,4096]{1,0:T(8,128)} %block.3, bf16[128,4096]{1,0:T(8,128)(2,1)} %get-tuple-element.21.halves), custom_call_target="tpu_custom_call" | custom-call | tf_op jit(solution)/shard_map/image_part/pallas_call | solution.py:483
  70.9 43.0 %images.1 = (f32[8,64,512]{2,1,0:T(8,128)}, f32[4,64,512]{2,1,0:T(8,128)}, f32[64,128]{1,0:T(8,128)}) custom-call(f32[4,64,512]{2,1,0:T(8,128)} %image_part.1.refs_0_, f32[64,4096]{1,0:T(8,128)} %get-tuple-element.22.refs_1_.refs_3_), custom_call_target="tpu_custom_call" | custom-call | tf_op jit(solution)/shard_map/images/pallas_call | solution.py:439
  113.8 5.5 %updates.1 = (bf16[2048,384]{1,0:T(8,128)(2,1)}, bf16[384,4096]{1,0:T(8,128)(2,1)}) custom-call(f32[64,128]{1,0:T(8,128)} %get-tuple-element.23.refs_0_, f32[64,64]{1,0:T(8,128)} %get-tuple-element.24.refs_1_, f32[64,64]{1,0:T(8,128)} %get-tuple-element.25.refs_2_, f32[64,4096]{1,0:T(8,128)} %get-tuple-element.22.refs_1_.refs_3_, ...), custom_call_target="tpu_custom_call" | custom-call | tf_op jit(solution)/shard_map/updates/pallas_call | solution.py:549
  119.4 24.5 %final.1 = f32[2048,4096]{1,0:T(8,128)} custom-call(f32[2048,4096]{1,0:T(8,128)} %block.3, bf16[2048,384]{1,0:T(8,128)(2,1)} %get-tuple-element.29.left, bf16[384,4096]{1,0:T(8,128)(2,1)} %get-tuple-element.30.right), custom_call_target="tpu_custom_call" | custom-call | tf_op jit(solution)/shard_map/final/pallas_call | solution.py:510
  (1 shorter events, 0.0 us)
where the time goes:
time: 145 us; the launch traced here: 144 us
  Pallas kernels  141 us (97%)
    pallas_call x1, Pallas kernels, images(): pl.pallas_call(lambda *refs: image_kernel(height, breadth, *refs), out_sh...  43 us
    pallas_call x1, Pallas kernels, spread(): pl.pallas_call(lambda *refs: spread_kernel(height, breadth, *refs), out_s...  35.6 us
    pallas_call x1, Pallas kernels, final(): pl.pallas_call(final_kernel, grid=(rows // tile,), out_shape=jax.ShapeDty...  24.5 us
    pallas_call x1, Pallas kernels, vectors_of(): pl.pallas_call(lambda *refs: vectors_kernel(height, breadth, *refs), out_...  17.6 us
    pallas_call x1, Pallas kernels, image_part(): pl.pallas_call(image_part_kernel, grid=(rows // width,), out_shape=jax.Sh...  15.3 us
    pallas_call x1, Pallas kernels, updates(): pl.pallas_call(lambda *refs: updates_kernel(height, breadth, *refs), out_...  5.54 us

commit v1 on v0

v1 whole, which is shorter than its diff:
```python
import jax
import jax.numpy as jnp
from jax import lax
from jax.experimental import pallas as pl
from jax.experimental.pallas import tpu as pltpu
from jax.sharding import PartitionSpec as P

B = 64
STEP = 8


highest = lax.Precision.HIGHEST
MESH = pl.DeviceIdType.MESH
f32 = jnp.float32
bf16 = jnp.bfloat16
NT = (((1,), (1,)), ((), ()))
TN = (((0,), (0,)), ((), ()))


def product(left, right):
    return jnp.dot(left, right, precision=highest, preferred_element_type=f32)


def product_nt(left, right):
    return lax.dot_general(left, right, NT, precision=highest, preferred_element_type=f32)


def product_tn(left, right):
    return lax.dot_general(left, right, TN, precision=highest, preferred_element_type=f32)


def split(x):
    upper = x.astype(bf16)
    return upper, (x - upper.astype(f32)).astype(bf16)


def eliminate(work, rows):
    for j in range(0, B, STEP):
        columns = [jnp.broadcast_to(work[:, j + k : j + k + 1], work.shape) for k in range(STEP)]
        lines = [work[j + k : j + k + 1, :] for k in range(STEP)]
        small = [[columns[c][j + r : j + r + 1, :] for c in range(STEP)] for r in range(STEP)]
        scaled = []
        for k in range(STEP):
            inverse = 1.0 / small[k][k]
            scaled.append(lines[k] * inverse)
            for m in range(k + 1, STEP):
                ratio = small[k][m] * inverse
                columns[m] = columns[m] - columns[k] * ratio
                lines[m] = lines[m] - lines[k] * ratio
                for c in range(m, STEP):
                    small[m][c] = small[m][c] - ratio * small[k][c]
        lowered = work
        for k in range(STEP):
            lowered = lowered - columns[k] * scaled[k]
        lowered = jnp.where(rows >= j + STEP, lowered, work)
        for k in range(1, STEP):
            lowered = jnp.where(rows == j + k, lines[k], lowered)
        work = lowered
    return work


def sign_inverse(q, rows):
    lane = lax.broadcasted_iota(jnp.int32, (1, 2 * B), 1)
    signs = jnp.zeros((B, 2 * B), f32)
    for j in range(0, B, STEP):
        columns = [jnp.broadcast_to(q[:, j + k : j + k + 1], q.shape) for k in range(STEP)]
        lines = [q[j + k : j + k + 1, :] for k in range(STEP)]
        small = [[columns[c][j + r : j + r + 1, :] for c in range(STEP)] for r in range(STEP)]
        scaled = []
        chosen = []
        for k in range(STEP):
            sign = jnp.where(small[k][k] >= 0, f32(-1.0), f32(1.0))
            pivot = small[k][k] - sign
            inverse = 1.0 / pivot
            chosen.append(sign)
            lines[k] = jnp.where(lane == j + k, pivot, lines[k]) * inverse
            scaled.append(lines[k])
            for c in range(k + 1, STEP):
                small[k][c] = small[k][c] * inverse
                columns[c] = columns[c] - columns[k] * small[k][c]
            for r in range(STEP):
                if r != k:
                    lines[r] = lines[r] - small[r][k] * lines[k]
                    for c in range(k + 1, STEP):
                        small[r][c] = small[r][c] - small[r][k] * small[k][c]
        for k in range(STEP):
            q = q - columns[k] * scaled[k]
        for k in range(STEP):
            q = jnp.where(rows == j + k, lines[k], q)
            signs = jnp.where(rows == j + k, chosen[k], signs)
    return q[:, B:], signs[:, :1]


def factor_values(gram, top):
    rows = lax.broadcasted_iota(jnp.int32, (B, 2 * B), 0)
    lanes = lax.broadcasted_iota(jnp.int32, (B, 2 * B), 1)
    small_rows = lax.broadcasted_iota(jnp.int32, (B, B), 0)
    small_lanes = lax.broadcasted_iota(jnp.int32, (B, B), 1)
    eye = jnp.where(small_rows == small_lanes, f32(1.0), f32(0.0))
    work = eliminate(jnp.concatenate([gram, eye], axis=1), rows)
    pivots = jnp.sum(jnp.where(rows == lanes, work, f32(0.0)), axis=1, keepdims=True)
    work = work * (1.0 / jnp.sqrt(pivots))
    upper = jnp.where(small_lanes >= small_rows, work[:, :B], f32(0.0))
    lower_inverse = work[:, B:]
    basis = product_nt(top, lower_inverse)
    inverse, signs = sign_inverse(jnp.concatenate([basis, eye], axis=1), rows)
    factor = -product_tn(lower_inverse, product(signs * inverse.T, lower_inverse))
    return factor, (signs * upper).T


def remote(src, dst, send_sem, recv_sem, device):
    return pltpu.make_async_remote_copy(
        src_ref=src,
        dst_ref=dst,
        send_sem=send_sem,
        recv_sem=recv_sem,
        device_id=device,
        device_id_type=MESH,
    )


def front_kernel(
    height, breadth, matrix, block, left, right,
    slab, strip, pc, pr, halves, own, parts, stats, chained, zs, rs, wr, wc, pe, ps, pt,
    local_sems, block_sems, pc_recvs, ring_sends, mate_sends, pr_recvs, pr_sends, part_sends, part_recvs,
    stat_sends, stat_recv, chain_send, chain_recv, rs_sends, rs_recvs, wr_right, wr_left, wr_recvs,
    role_send, wc_recvs, wc_sends, pe_sends, pe_recvs, pt_sends, pt_recvs,
):
    r, c = lax.axis_index("row"), lax.axis_index("col")
    rows, cols = matrix.shape
    width = cols // height
    half = height // 2
    count = height * breadth
    me = r * breadth + c
    core = lax.rem(r, 2)
    chip = r // 2
    even = core == 0
    odd = core == 1
    mate = r + 1 - 2 * core
    place = 2 * (chip // 2) + lax.rem(lax.rem(chip, 2) + chip // 2, 2)

    def seat(q):
        return 2 * (2 * (q // 2) + lax.rem(q + q // 2, 2))

    root = r == 0
    edge = c == 0

    slab_copy = pltpu.make_async_copy(matrix.at[pl.ds(0, B)], slab, local_sems.at[0])
    strip_copy = pltpu.make_async_copy(matrix.at[:, pl.ds(0, 2 * B)], strip, local_sems.at[1])
    pl.when(root)(slab_copy.start)
    pl.when(edge)(strip_copy.start)
    block_copies = []
    for k in range(breadth):
        part = pl.ds(k * width, width)
        block_copies.append(pltpu.make_async_copy(matrix.at[part], block.at[part], block_sems.at[k]))
        block_copies[-1].start()

    barrier = pltpu.get_barrier_semaphore()

    def greet(step, carry):
        other = lax.rem(me + step, count)
        pl.semaphore_signal(
            barrier, inc=1, device_id=(other // breadth, lax.rem(other, breadth)), device_id_type=MESH
        )
        return carry

    lax.fori_loop(1, count, greet, 0)

    @pl.when(root)
    def _():
        slab_copy.wait()
        lane = lax.broadcasted_iota(jnp.int32, (B, cols), 1) + c * cols
        panel = jnp.where(lane >= B, slab[...], f32(0.0))
        for i in range(height):
            pc[i] = panel[:, i * width : (i + 1) * width]
        top = jnp.where(edge, slab[:, B : 2 * B], f32(0.0))
        own[...] = jnp.concatenate([product_nt(panel, panel), top], axis=1)

    pl.semaphore_wait(barrier, count - 1)

    def ring_copy(i, target):
        return remote(pc.at[i], pc.at[i], ring_sends.at[i], pc_recvs.at[i], (target, c))

    def mate_copy(i):
        return remote(pc.at[i], pc.at[i], mate_sends.at[i], pc_recvs.at[i], (mate, c))

    def part_copy(k):
        return remote(own, parts.at[c], part_sends.at[k], part_recvs.at[c], (1, k))

    forth = seat(lax.rem(place + 1, half))
    back = seat(lax.rem(place + half - 1, half))
    goes_forth = place + 1 < half
    goes_back = place != 1

    def ring_on(i):
        if i < half:
            pl.when(goes_forth)(ring_copy(i, forth).start)
        else:
            pl.when(goes_back)(ring_copy(i, back).start)

    def passed(i):
        remote(pc.at[i], pc.at[i], ring_sends.at[i], pc_recvs.at[i], (mate, c)).wait_recv()
        ring_on(i)
        mate_copy(i).start()

    @pl.when(root)
    def _():
        for k in range(breadth):
            part_copy(k).start()
        for i in range(half):
            ring_copy(i, forth).start()
            ring_copy(half + i, back).start()
        for i in range(height):
            mate_copy(i).start()

    def line_copy(k):
        return remote(pr.at[k], pr.at[k], pr_sends.at[k], pr_recvs.at[k], (r, c + 1))

    def line_received(k):
        remote(pr.at[k], pr.at[k], pr_sends.at[k], pr_recvs.at[k], (r, 0)).wait_recv()

    @pl.when(edge)
    def _():
        strip_copy.wait()
        for k in range(breadth - 1, -1, -1):
            piece = strip[k * width : (k + 1) * width, :].T[:B, :]
            lane = lax.broadcasted_iota(jnp.int32, (B, width), 1) + r * rows + k * width
            pr[k] = jnp.where(lane >= B, piece, f32(0.0))
            line_copy(k).start()

    middle = jnp.logical_and(c >= 1, c < breadth - 1)

    def line_pass(point):
        index = point - 2 * (c - 1)
        k = breadth - 1 - index

        @pl.when(jnp.logical_and(middle, jnp.logical_and(index >= 0, index < breadth)))
        def _():
            line_received(k)
            line_copy(k).start()

    relays = jnp.logical_and(even, jnp.logical_not(root))

    @pl.when(jnp.logical_and(relays, 2 * place < half))
    def _():
        for i in range(height):
            passed(i)

    @pl.when(jnp.logical_and(relays, 2 * place == half))
    def _():
        for i in range(half):
            passed(i)
            passed(half + i)

    @pl.when(jnp.logical_and(relays, 2 * place > half))
    def _():
        for i in range(height):
            passed((half + i) % height)

    def stat_copy(q):
        return remote(stats, stats, stat_sends.at[q], stat_recv, (2 * q + 1, c))

    chain_copy = remote(chained, chained, chain_send, chain_recv, (mate, c))

    @pl.when(r == 1)
    def _():
        total = None
        for k in range(breadth):
            remote(parts.at[k], parts.at[k], part_sends.at[k], part_recvs.at[k], (0, c)).wait_recv()
            total = parts[k] if total is None else total + parts[k]
        stats[...] = total
        for q in range(1, half):
            stat_copy(q).start()

    @pl.when(jnp.logical_and(odd, r != 1))
    def _():
        remote(stats, stats, stat_sends.at[0], stat_recv, (1, c)).wait_recv()

    @pl.when(odd)
    def _():
        factor, turned = factor_values(stats[:, :B], stats[:, B:].T)
        chained[...] = jnp.concatenate([factor, turned], axis=1)
        chain_copy.start()
        for i in range(height):
            remote(pc.at[i], pc.at[i], mate_sends.at[i], pc_recvs.at[i], (mate, c)).wait_recv()

    @pl.when(even)
    def _():
        for i in range(height):
            mate_copy(i).wait_send()
        chain_copy.wait_recv()

    @pl.when(root)
    def _():
        for i in range(half):
            ring_copy(i, forth).wait_send()
            ring_copy(half + i, back).wait_send()

    @pl.when(relays)
    def _():
        for i in range(half):
            pl.when(goes_forth)(ring_copy(i, forth).wait_send)
            pl.when(goes_back)(ring_copy(half + i, back).wait_send)

    def lower_top(buffer):
        for i in range(buffer.shape[0]):
            low, high = max(B, i * width), min(2 * B, (i + 1) * width)
            if low < high:
                lanes = slice(low - i * width, high - i * width)
                buffer[i, :, lanes] = buffer[i, :, lanes] - chained[:, low : high]

    @pl.when(edge)
    def _():
        lower_top(pc)

    for i in range(height):
        part = slice(i * width, (i + 1) * width)
        upper, lower = split(pc[i])
        halves[:B, part] = upper
        halves[B:, part] = lower
    for copy in block_copies:
        copy.wait()

    size = min(512, cols)

    def rs_copy(step, other):
        return remote(zs.at[other], rs.at[c], rs_sends.at[step], rs_recvs.at[c], (r, other))

    order = sorted(range(1, breadth), key=lambda s: -min(s, breadth - s)) + [0]
    for index, step in enumerate(order):
        line_pass(index)
        other = lax.rem(c + step, breadth)
        some = pl.ds(pl.multiple_of(other * width, width), width)
        both = jnp.zeros((width, 2 * B), f32)
        for start in range(0, cols, size):
            part = slice(start, start + size)
            upper, lower = split(block[some, part])
            both = both + lax.dot_general(upper, halves[:, part], NT, preferred_element_type=f32)
            low = lax.dot_general(lower, halves[:, part], NT, preferred_element_type=f32)
            both = both + jnp.where(lax.broadcasted_iota(jnp.int32, both.shape, 1) < B, low, f32(0.0))
        turned = both.T
        value = turned[:B, :] + turned[B:, :]
        if step:
            zs[other] = value
            rs_copy(step, other).start()
        else:
            rs[c] = value
    for index in range(breadth, breadth + 2 * max(0, breadth - 3)):
        line_pass(index)

    for step in range(1, breadth):
        other = lax.rem(c + step, breadth)
        remote(rs.at[other], rs.at[other], rs_sends.at[step], rs_recvs.at[other], (r, other)).wait_recv()
    total = rs[0]
    for k in range(1, breadth):
        total = total + rs[k]
    wr[c] = total

    def right_copy(k):
        return remote(wr.at[k], wr.at[k], wr_right.at[k], wr_recvs.at[k], (r, c + 1))

    def left_copy(k):
        return remote(wr.at[k], wr.at[k], wr_left.at[k], wr_recvs.at[k], (r, c - 1))

    has_right = c + 1 < breadth
    has_left = c >= 1
    to_row = lax.rem(me, height)
    to_col = me // height
    itself = jnp.logical_and(to_row == r, to_col == c)
    role = remote(wr.at[c], wc.at[to_row], role_send, wc_recvs.at[to_row], (to_row, to_col))
    pl.when(has_right)(right_copy(c).start)
    pl.when(has_left)(left_copy(c).start)
    pl.when(jnp.logical_not(itself))(role.start)

    @pl.when(itself)
    def _():
        wc[r] = total

    @pl.when(c == breadth - 1)
    def _():
        line_received(breadth - 1)

    slots = lax.broadcasted_iota(jnp.int32, (B, width), 0)
    positions = lax.broadcasted_iota(jnp.int32, (B, width), 1) + me * width - B
    onehot = jnp.where(positions == slots, f32(1.0), f32(0.0))
    vector = pr[c] - product(chained[:, B:], onehot)
    pe[r] = jnp.concatenate([product_nt(total, vector), jnp.zeros((B, B), f32)], axis=1)

    def pe_copy(step):
        other = lax.rem(r + step, height)
        return remote(pe.at[r], pe.at[r], pe_sends.at[step], pe_recvs.at[r], (other, c)), other

    for step in range(1, height):
        pe_copy(step)[0].start()

    def wr_pass(s):
        @pl.when(c - s >= 0)
        def _():
            remote(wr.at[c - s], wr.at[c - s], wr_right.at[0], wr_recvs.at[c - s], (r, c - 1)).wait_recv()
            pl.when(has_right)(right_copy(c - s).start)

        @pl.when(c + s < breadth)
        def _():
            remote(wr.at[c + s], wr.at[c + s], wr_left.at[0], wr_recvs.at[c + s], (r, c + 1)).wait_recv()
            pl.when(has_left)(left_copy(c + s).start)

    def wc_copy(slot, step, other):
        return remote(wc.at[slot], wc.at[slot], wc_sends.at[step], wc_recvs.at[slot], (other, c))

    def wc_received(slot):
        remote(wc.at[slot], wc.at[slot], wc_sends.at[0], wc_recvs.at[slot], (mate, c)).wait_recv()

    pl.when(jnp.logical_not(itself))(lambda: wc_received(r))
    for step in range(2, height, 2):
        wc_copy(r, step, lax.rem(r + step, height)).start()
    wc_copy(r, 1, mate).start()
    wr_pass(1)
    summed = pe[r]
    for step in range(1, height):
        copy, other = pe_copy(step)
        remote(pe.at[other], pe.at[other], pe_sends.at[step], pe_recvs.at[other], (other, c)).wait_recv()
        summed = summed + pe[other]
    ps[c] = summed

    def ps_copy(step):
        other = lax.rem(c + step, breadth)
        return remote(ps.at[c], ps.at[c], pt_sends.at[step], pt_recvs.at[c], (r, other)), other

    for step in range(1, breadth):
        ps_copy(step)[0].start()
    for step in range(2, height, 2):
        slot = lax.rem(r + step, height)
        wc_received(slot)
        wc_copy(slot, step + 1, mate).start()
    for s in range(2, breadth):
        wr_pass(s)
    projected = ps[c]
    for step in range(1, breadth):
        copy, other = ps_copy(step)
        remote(ps.at[other], ps.at[other], pt_sends.at[step], pt_recvs.at[other], (r, other)).wait_recv()
        projected = projected + ps[other]

    factor = chained[:, :B]
    turned = factor.T
    inner = product(turned, product(projected[:, :B], factor))
    mix = jnp.concatenate([turned, -0.5 * inner], axis=1)
    wc_received(mate)
    for step in range(2, height, 2):
        wc_received(lax.rem(mate + step, height))
    for i in range(height):
        part = slice(i * width, (i + 1) * width)
        v = pc[i]
        u = product(mix, jnp.concatenate([wc[i], v], axis=0))
        upper, lower = split(jnp.concatenate([u, v], axis=0))
        right[: 2 * B, part] = upper
        right[2 * B : 4 * B, part] = upper
        right[4 * B :, part] = lower

    @pl.when(c == breadth - 1)
    def _():
        for k in range(breadth - 1):
            line_received(k)

    @pl.when(c < breadth - 1)
    def _():
        for k in range(breadth):
            line_copy(k).wait_send()

    @pl.when(root)
    def _():
        lower_top(pr)

    for i in range(breadth):
        part = slice(i * width, (i + 1) * width)
        v = pr[i]
        u = product(mix, jnp.concatenate([wr[i], v], axis=0))
        upper, lower = split(jnp.concatenate([v, u], axis=0).T)
        left[part, : 2 * B] = upper
        left[part, 2 * B : 4 * B] = lower
        left[part, 4 * B :] = upper

    @pl.when(root)
    def _():
        for k in range(breadth):
            part_copy(k).wait_send()

    @pl.when(r == 1)
    def _():
        for q in range(1, half):
            stat_copy(q).wait_send()

    pl.when(odd)(chain_copy.wait_send)
    for step in range(1, breadth):
        rs_copy(step, lax.rem(c + step, breadth)).wait_send()
        ps_copy(step)[0].wait_send()
    for step in range(1, height):
        pe_copy(step)[0].wait_send()
    pl.when(jnp.logical_not(itself))(role.wait_send)
    for step in range(2, height, 2):
        wc_copy(r, step, lax.rem(r + step, height)).wait_send()
        wc_copy(lax.rem(r + step, height), step + 1, mate).wait_send()
    wc_copy(r, 1, mate).wait_send()

    @pl.when(has_right)
    def _():
        for k in range(breadth):
            pl.when(k <= c)(right_copy(k).wait_send)

    @pl.when(has_left)
    def _():
        for k in range(breadth):
            pl.when(k >= c)(left_copy(k).wait_send)


def front(matrix, height, breadth):
    rows, cols = matrix.shape
    width = cols // height
    vmem = pl.BlockSpec(memory_space=pltpu.VMEM)
    dma = pltpu.SemaphoreType.DMA
    scratch = [
        pltpu.VMEM((B, cols), f32),
        pltpu.VMEM((rows, 2 * B), f32),
        pltpu.VMEM((height, B, width), f32),
        pltpu.VMEM((breadth, B, width), f32),
        pltpu.VMEM((2 * B, cols), bf16),
        pltpu.VMEM((B, 2 * B), f32),
        pltpu.VMEM((breadth, B, 2 * B), f32),
        pltpu.VMEM((B, 2 * B), f32),
        pltpu.VMEM((B, 2 * B), f32),
        pltpu.VMEM((breadth, B, width), f32),
        pltpu.VMEM((breadth, B, width), f32),
        pltpu.VMEM((breadth, B, width), f32),
        pltpu.VMEM((height, B, width), f32),
        pltpu.VMEM((height, B, 2 * B), f32),
        pltpu.VMEM((breadth, B, 2 * B), f32),
        pltpu.VMEM((B, 2 * B), f32),
        dma((2,)),
        dma((breadth,)),
        dma((height,)),
        dma((height,)),
        dma((height,)),
        dma((breadth,)),
        dma((breadth,)),
        dma((breadth,)),
        dma((breadth,)),
        dma((height // 2,)),
        dma(()),
        dma(()),
        dma(()),
        dma((breadth,)),
        dma((breadth,)),
        dma((breadth,)),
        dma((breadth,)),
        dma((breadth,)),
        dma(()),
        dma((height,)),
        dma((height,)),
        dma((height,)),
        dma((height,)),
        dma((breadth,)),
        dma((breadth,)),
    ]
    return pl.pallas_call(
        lambda *refs: front_kernel(height, breadth, *refs),
        out_shape=[
            pltpu.VMEM((rows, cols), f32),
            pltpu.VMEM((rows, 6 * B), bf16),
            pltpu.VMEM((6 * B, cols), bf16),
        ],
        in_specs=[pl.BlockSpec(memory_space=pl.ANY)],
        out_specs=[vmem] * 3,
        scratch_shapes=scratch,
        compiler_params=pltpu.CompilerParams(
            collective_id=0, has_side_effects=True, vmem_limit_bytes=20 << 20
        ),
        name="front",
    )(matrix)


def final_kernel(tile, slots, block, left, right, out, buffer, sems):
    rows, cols = block.shape
    size = min(512, cols)
    count = rows // tile

    def copy(i):
        return pltpu.make_async_copy(
            buffer.at[i % slots], out.at[pl.ds(i * tile, tile)], sems.at[i % slots]
        )

    for i in range(count):
        if i >= slots:
            copy(i - slots).wait()
        some = slice(i * tile, (i + 1) * tile)
        for start in range(0, cols, size):
            part = slice(start, start + size)
            buffer[i % slots, :, part] = block[some, part] - jnp.dot(
                left[some, :], right[:, part], preferred_element_type=f32
            )
        copy(i).start()
    for i in range(max(0, count - slots), count):
        copy(i).wait()


def final(block, left, right):
    rows, cols = block.shape
    tile = min(256, rows)
    slots = min(4, rows // tile)
    vmem = pl.BlockSpec(memory_space=pltpu.VMEM)
    held = [pltpu.with_memory_space_constraint(x, pltpu.VMEM) for x in (block, left, right)]
    return pl.pallas_call(
        lambda *refs: final_kernel(tile, slots, *refs),
        out_shape=jax.ShapeDtypeStruct((rows, cols), f32),
        in_specs=[vmem] * 3,
        out_specs=pl.BlockSpec(memory_space=pl.ANY),
        scratch_shapes=[
            pltpu.VMEM((slots, tile, cols), f32),
            pltpu.SemaphoreType.DMA((slots,)),
        ],
        compiler_params=pltpu.CompilerParams(vmem_limit_bytes=20 << 20),
        name="final",
    )(*held)


def solution(mesh):
    height, breadth = mesh.shape["row"], mesh.shape["col"]

    def shards(matrix):
        return final(*front(matrix, height, breadth))

    return jax.shard_map(
        shards,
        mesh=mesh,
        in_specs=(P("row", "col"),),
        out_specs=P("row", "col"),
        check_vma=False,
    )
```

time: 145 us -> 92.1 us (0.64)
  the two profiles are of different devices: /device:TPU:4 before, /device:TPU:25 now
where the time goes in v1:
time: 92.1 us; the launch traced here: 92 us
  Pallas kernels  91.8 us (100%)
    pallas_call x1, Pallas kernels, front(): pl.pallas_call(lambda *refs: front_kernel(height, breadth, *refs), out_sh...  79.5 us
    pallas_call x1, Pallas kernels, final(): pl.pallas_call(lambda *refs: final_kernel(tile, slots, *refs), out_shape=...  12.2 us

profile of v1, /device:TPU:25, one launch (start us, length us, event | category | flops | bytes accessed | tf_op | source)
XLA Modules:
  0.0 92.0 jit_solution(14449402601649980396)
XLA Ops:
  0.0 79.5 %front.1 = (f32[2048,4096]{1,0:T(8,128)S(1)}, bf16[2048,384]{1,0:T(8,128)(2,1)S(1)}, bf16[384,4096]{1,0:T(8,128)(2,1)S(1)}) custom-call(f32[2048,4096]{1,0:T(8,128)} %refs_0_.1), custom_call_target="tpu_custom_call" | custom-call | tf_op jit(solution)/shard_map/front/pallas_call | solution.py:563
  79.5 12.2 %final.1 = f32[2048,4096]{1,0:T(8,128)} custom-call(f32[2048,4096]{1,0:T(8,128)S(1)} %get-tuple-element.8.refs_0_, bf16[2048,384]{1,0:T(8,128)(2,1)S(1)} %get-tuple-element.9.refs_1_, bf16[384,4096]{1,0:T(8,128)(2,1)S(1)} %get-tuple-element.10.refs_2_), custom_call_target="tpu_custom_call" | custom-call | tf_op jit(solution)/shard_map/final/pallas_call | solution.py:610

commit v2 on v1

--- a/solution.py
+++ b/solution.py
@@ -153,7 +153,6 @@
     for k in range(breadth):
         part = pl.ds(k * width, width)
         block_copies.append(pltpu.make_async_copy(matrix.at[part], block.at[part], block_sems.at[k]))
-        block_copies[-1].start()
 
     barrier = pltpu.get_barrier_semaphore()
 
@@ -166,23 +165,45 @@
 
     lax.fori_loop(1, count, greet, 0)
 
+    def masked_slab():
+        lane = lax.broadcasted_iota(jnp.int32, (B, cols), 1) + c * cols
+        return jnp.where(lane >= B, slab[...], f32(0.0))
+
     @pl.when(root)
     def _():
         slab_copy.wait()
-        lane = lax.broadcasted_iota(jnp.int32, (B, cols), 1) + c * cols
-        panel = jnp.where(lane >= B, slab[...], f32(0.0))
+        panel = masked_slab()
         for i in range(height):
             pc[i] = panel[:, i * width : (i + 1) * width]
+
+    pl.when(edge)(strip_copy.wait)
+    for copy in block_copies:
+        copy.start()
+
+    @pl.when(root)
+    def _():
+        panel = masked_slab()
         top = jnp.where(edge, slab[:, B : 2 * B], f32(0.0))
         own[...] = jnp.concatenate([product_nt(panel, panel), top], axis=1)
 
+    @pl.when(edge)
+    def _():
+        for k in range(breadth):
+            piece = strip[k * width : (k + 1) * width, :].T[:B, :]
+            lane = lax.broadcasted_iota(jnp.int32, (B, width), 1) + r * rows + k * width
+            pr[k] = jnp.where(lane >= B, piece, f32(0.0))
+
     pl.semaphore_wait(barrier, count - 1)
 
-    def ring_copy(i, target):
-        return remote(pc.at[i], pc.at[i], ring_sends.at[i], pc_recvs.at[i], (target, c))
-
-    def mate_copy(i):
-        return remote(pc.at[i], pc.at[i], mate_sends.at[i], pc_recvs.at[i], (mate, c))
+    def piece_copy(i, part, sends, target):
+        some = pc.at[i, pl.ds(part * (B // 2), B // 2)]
+        return remote(some, some, sends.at[i, part], pc_recvs.at[i, part], (target, c))
+
+    def ring_copy(i, part, target):
+        return piece_copy(i, part, ring_sends, target)
+
+    def mate_copy(i, part):
+        return piece_copy(i, part, mate_sends, mate)
 
     def part_copy(k):
         return remote(own, parts.at[c], part_sends.at[k], part_recvs.at[c], (1, k))
@@ -192,26 +213,28 @@
     goes_forth = place + 1 < half
     goes_back = place != 1
 
-    def ring_on(i):
+    def ring_on(i, part):
         if i < half:
-            pl.when(goes_forth)(ring_copy(i, forth).start)
+            pl.when(goes_forth)(ring_copy(i, part, forth).start)
         else:
-            pl.when(goes_back)(ring_copy(i, back).start)
-
-    def passed(i):
-        remote(pc.at[i], pc.at[i], ring_sends.at[i], pc_recvs.at[i], (mate, c)).wait_recv()
-        ring_on(i)
-        mate_copy(i).start()
+            pl.when(goes_back)(ring_copy(i, part, back).start)
+
+    def passed(i, part):
+        mate_copy(i, part).wait_recv()
+        ring_on(i, part)
+        mate_copy(i, part).start()
 
     @pl.when(root)
     def _():
         for k in range(breadth):
             part_copy(k).start()
         for i in range(half):
-            ring_copy(i, forth).start()
-            ring_copy(half + i, back).start()
+            for part in range(2):
+                ring_copy(i, part, forth).start()
+                ring_copy(half + i, part, back).start()
         for i in range(height):
-            mate_copy(i).start()
+            for part in range(2):
+                mate_copy(i, part).start()
 
     def line_copy(k):
         return remote(pr.at[k], pr.at[k], pr_sends.at[k], pr_recvs.at[k], (r, c + 1))
@@ -221,41 +244,47 @@
 
     @pl.when(edge)
     def _():
-        strip_copy.wait()
         for k in range(breadth - 1, -1, -1):
-            piece = strip[k * width : (k + 1) * width, :].T[:B, :]
-            lane = lax.broadcasted_iota(jnp.int32, (B, width), 1) + r * rows + k * width
-            pr[k] = jnp.where(lane >= B, piece, f32(0.0))
             line_copy(k).start()
 
     middle = jnp.logical_and(c >= 1, c < breadth - 1)
 
-    def line_pass(point):
-        index = point - 2 * (c - 1)
+    def line_pass(who, index):
         k = breadth - 1 - index
 
-        @pl.when(jnp.logical_and(middle, jnp.logical_and(index >= 0, index < breadth)))
+        @pl.when(jnp.logical_and(middle, c == who))
         def _():
             line_received(k)
             line_copy(k).start()
 
     relays = jnp.logical_and(even, jnp.logical_not(root))
 
+    def go_round(pieces):
+        for step, (i, part) in enumerate(pieces):
+            passed(i, part)
+            for index in range(breadth):
+                if (index + 1) * len(pieces) // breadth - 1 == step:
+                    line_pass(1, index)
+
+    pieces = [(i, part) for i in range(height) for part in range(2)]
+    later = pieces[height:] + pieces[:height]
+
     @pl.when(jnp.logical_and(relays, 2 * place < half))
     def _():
-        for i in range(height):
-            passed(i)
+        go_round(pieces)
 
     @pl.when(jnp.logical_and(relays, 2 * place == half))
     def _():
-        for i in range(half):
-            passed(i)
-            passed(half + i)
+        go_round([piece for pair in zip(pieces[:height], later[:height]) for piece in pair])
 
     @pl.when(jnp.logical_and(relays, 2 * place > half))
     def _():
-        for i in range(height):
-            passed((half + i) % height)
+        go_round(later)
+
+    @pl.when(root)
+    def _():
+        for index in range(breadth):
+            line_pass(1, index)
 
     def stat_copy(q):
         return remote(stats, stats, stat_sends.at[q], stat_recv, (2 * q + 1, c))
@@ -272,6 +301,8 @@
         for q in range(1, half):
             stat_copy(q).start()
 
+    pl.when(odd)(lambda: line_pass(1, 0))
+
     @pl.when(jnp.logical_and(odd, r != 1))
     def _():
         remote(stats, stats, stat_sends.at[0], stat_recv, (1, c)).wait_recv()
@@ -281,26 +312,28 @@
         factor, turned = factor_values(stats[:, :B], stats[:, B:].T)
         chained[...] = jnp.concatenate([factor, turned], axis=1)
         chain_copy.start()
-        for i in range(height):
-            remote(pc.at[i], pc.at[i], mate_sends.at[i], pc_recvs.at[i], (mate, c)).wait_recv()
+        for index in range(1, breadth):
+            line_pass(1, index)
+        for i, part in pieces:
+            mate_copy(i, part).wait_recv()
 
     @pl.when(even)
     def _():
-        for i in range(height):
-            mate_copy(i).wait_send()
+        for i, part in pieces:
+            mate_copy(i, part).wait_send()
         chain_copy.wait_recv()
 
     @pl.when(root)
     def _():
-        for i in range(half):
-            ring_copy(i, forth).wait_send()
-            ring_copy(half + i, back).wait_send()
+        for i, part in pieces[:height]:
+            ring_copy(i, part, forth).wait_send()
+            ring_copy(half + i, part, back).wait_send()
 
     @pl.when(relays)
     def _():
-        for i in range(half):
-            pl.when(goes_forth)(ring_copy(i, forth).wait_send)
-            pl.when(goes_back)(ring_copy(half + i, back).wait_send)
+        for i, part in pieces[:height]:
+            pl.when(goes_forth)(ring_copy(i, part, forth).wait_send)
+            pl.when(goes_back)(ring_copy(half + i, part, back).wait_send)
 
     def lower_top(buffer):
         for i in range(buffer.shape[0]):
@@ -328,7 +361,10 @@
 
     order = sorted(range(1, breadth), key=lambda s: -min(s, breadth - s)) + [0]
     for index, step in enumerate(order):
-        line_pass(index)
+        if index < 3:
+            bounds = [0, breadth // 2, 3 * breadth // 4, breadth]
+            for k in range(bounds[index], bounds[index + 1]):
+                line_pass(2, k)
         other = lax.rem(c + step, breadth)
         some = pl.ds(pl.multiple_of(other * width, width), width)
         both = jnp.zeros((width, 2 * B), f32)
@@ -345,8 +381,9 @@
             rs_copy(step, other).start()
         else:
             rs[c] = value
-    for index in range(breadth, breadth + 2 * max(0, breadth - 3)):
-        line_pass(index)
+    for who in range(3, breadth - 1):
+        for k in range(breadth):
+            line_pass(who, k)
 
     for step in range(1, breadth):
         other = lax.rem(c + step, breadth)
@@ -536,9 +573,9 @@
         pltpu.VMEM((B, 2 * B), f32),
         dma((2,)),
         dma((breadth,)),
-        dma((height,)),
-        dma((height,)),
-        dma((height,)),
+        dma((height, 2)),
+        dma((height, 2)),
+        dma((height, 2)),
         dma((breadth,)),
         dma((breadth,)),
         dma((breadth,)),

time: 92.1 us -> 76.6 us (0.83)
  the two profiles are of different devices: /device:TPU:25 before, /device:TPU:0 now
where the time goes in v2:
time: 76.6 us; the launch traced here: 76.5 us
  Pallas kernels  76.3 us (100%)
    pallas_call x1, Pallas kernels, front(): pl.pallas_call(lambda *refs: front_kernel(height, breadth, *refs), out_sh...  64 us
    pallas_call x1, Pallas kernels, final(): pl.pallas_call(lambda *refs: final_kernel(tile, slots, *refs), out_shape=...  12.2 us

profile of v2, /device:TPU:0, one launch (start us, length us, event | category | flops | bytes accessed | tf_op | source)
XLA Modules:
  0.0 76.5 jit_solution(14928528072558852315)
XLA Ops:
  0.0 64.0 %front.1 = (f32[2048,4096]{1,0:T(8,128)S(1)}, bf16[2048,384]{1,0:T(8,128)(2,1)S(1)}, bf16[384,4096]{1,0:T(8,128)(2,1)S(1)}) custom-call(f32[2048,4096]{1,0:T(8,128)} %refs_0_.1), custom_call_target="tpu_custom_call" | custom-call | tf_op jit(solution)/shard_map/front/pallas_call | solution.py:600
  64.0 12.2 %final.1 = f32[2048,4096]{1,0:T(8,128)} custom-call(f32[2048,4096]{1,0:T(8,128)S(1)} %get-tuple-element.8.refs_0_, bf16[2048,384]{1,0:T(8,128)(2,1)S(1)} %get-tuple-element.9.refs_1_, bf16[384,4096]{1,0:T(8,128)(2,1)S(1)} %get-tuple-element.10.refs_2_), custom_call_target="tpu_custom_call" | custom-call | tf_op jit(solution)/shard_map/final/pallas_call | solution.py:647

commit v3 on v2

--- a/solution.py
+++ b/solution.py
@@ -249,10 +249,10 @@
 
     middle = jnp.logical_and(c >= 1, c < breadth - 1)
 
-    def line_pass(who, index):
+    def line_pass(who, index, when=True):
         k = breadth - 1 - index
 
-        @pl.when(jnp.logical_and(middle, c == who))
+        @pl.when(jnp.logical_and(jnp.logical_and(middle, c == who), when))
         def _():
             line_received(k)
             line_copy(k).start()
@@ -361,10 +361,13 @@
 
     order = sorted(range(1, breadth), key=lambda s: -min(s, breadth - s)) + [0]
     for index, step in enumerate(order):
-        if index < 3:
-            bounds = [0, breadth // 2, 3 * breadth // 4, breadth]
-            for k in range(bounds[index], bounds[index + 1]):
-                line_pass(2, k)
+        for k in range(breadth):
+            early = max(0, k - breadth // 4)
+            late = min(breadth - 1, breadth - 2 + k // 2)
+            if 4 * early // breadth == index:
+                line_pass(2, k, r >= 2)
+            if late == index:
+                line_pass(2, k, r < 2)
         other = lax.rem(c + step, breadth)
         some = pl.ds(pl.multiple_of(other * width, width), width)
         both = jnp.zeros((width, 2 * B), f32)
@@ -393,11 +396,15 @@
         total = total + rs[k]
     wr[c] = total
 
-    def right_copy(k):
-        return remote(wr.at[k], wr.at[k], wr_right.at[k], wr_recvs.at[k], (r, c + 1))
-
-    def left_copy(k):
-        return remote(wr.at[k], wr.at[k], wr_left.at[k], wr_recvs.at[k], (r, c - 1))
+    def sum_copy(k, part, sends, target):
+        some = wr.at[k, pl.ds(part * (B // 2), B // 2)]
+        return remote(some, some, sends.at[k, part], wr_recvs.at[k, part], (r, target))
+
+    def right_copy(k, part):
+        return sum_copy(k, part, wr_right, c + 1)
+
+    def left_copy(k, part):
+        return sum_copy(k, part, wr_left, c - 1)
 
     has_right = c + 1 < breadth
     has_left = c >= 1
@@ -405,9 +412,10 @@
     to_col = me // height
     itself = jnp.logical_and(to_row == r, to_col == c)
     role = remote(wr.at[c], wc.at[to_row], role_send, wc_recvs.at[to_row], (to_row, to_col))
-    pl.when(has_right)(right_copy(c).start)
-    pl.when(has_left)(left_copy(c).start)
     pl.when(jnp.logical_not(itself))(role.start)
+    for part in range(2):
+        pl.when(has_right)(right_copy(c, part).start)
+        pl.when(has_left)(left_copy(c, part).start)
 
     @pl.when(itself)
     def _():
@@ -431,15 +439,17 @@
         pe_copy(step)[0].start()
 
     def wr_pass(s):
-        @pl.when(c - s >= 0)
-        def _():
-            remote(wr.at[c - s], wr.at[c - s], wr_right.at[0], wr_recvs.at[c - s], (r, c - 1)).wait_recv()
-            pl.when(has_right)(right_copy(c - s).start)
-
-        @pl.when(c + s < breadth)
-        def _():
-            remote(wr.at[c + s], wr.at[c + s], wr_left.at[0], wr_recvs.at[c + s], (r, c + 1)).wait_recv()
-            pl.when(has_left)(left_copy(c + s).start)
+        for part in range(2):
+
+            @pl.when(c - s >= 0)
+            def _():
+                sum_copy(c - s, part, wr_right, c - 1).wait_recv()
+                pl.when(has_right)(right_copy(c - s, part).start)
+
+            @pl.when(c + s < breadth)
+            def _():
+                sum_copy(c + s, part, wr_left, c + 1).wait_recv()
+                pl.when(has_left)(left_copy(c + s, part).start)
 
     def wc_copy(slot, step, other):
         return remote(wc.at[slot], wc.at[slot], wc_sends.at[step], wc_recvs.at[slot], (other, c))
@@ -465,12 +475,14 @@
 
     for step in range(1, breadth):
         ps_copy(step)[0].start()
+    for s in range(2, breadth - 1):
+        wr_pass(s)
     for step in range(2, height, 2):
         slot = lax.rem(r + step, height)
         wc_received(slot)
         wc_copy(slot, step + 1, mate).start()
-    for s in range(2, breadth):
-        wr_pass(s)
+    if breadth > 2:
+        wr_pass(breadth - 1)
     projected = ps[c]
     for step in range(1, breadth):
         copy, other = ps_copy(step)
@@ -541,12 +553,14 @@
     @pl.when(has_right)
     def _():
         for k in range(breadth):
-            pl.when(k <= c)(right_copy(k).wait_send)
+            for part in range(2):
+                pl.when(k <= c)(right_copy(k, part).wait_send)
 
     @pl.when(has_left)
     def _():
         for k in range(breadth):
-            pl.when(k >= c)(left_copy(k).wait_send)
+            for part in range(2):
+                pl.when(k >= c)(left_copy(k, part).wait_send)
 
 
 def front(matrix, height, breadth):
@@ -586,9 +600,9 @@
         dma(()),
         dma((breadth,)),
         dma((breadth,)),
-        dma((breadth,)),
-        dma((breadth,)),
-        dma((breadth,)),
+        dma((breadth, 2)),
+        dma((breadth, 2)),
+        dma((breadth, 2)),
         dma(()),
         dma((height,)),
         dma((height,)),

time: 76.6 us -> 72.6 us (0.948)
  the two profiles are of different devices: /device:TPU:0 before, /device:TPU:4 now
where the time goes in v3:
time: 72.6 us; the launch traced here: 72 us
  Pallas kernels  71.8 us (99%)
    pallas_call x1, Pallas kernels, front(): pl.pallas_call(lambda *refs: front_kernel(height, breadth, *refs), out_sh...  59.6 us
    pallas_call x1, Pallas kernels, final(): pl.pallas_call(lambda *refs: final_kernel(tile, slots, *refs), out_shape=...  12.2 us

profile of v3, /device:TPU:4, one launch (start us, length us, event | category | flops | bytes accessed | tf_op | source)
XLA Modules:
  0.0 72.0 jit_solution(16900983019081261101)
XLA Ops:
  0.0 59.6 %front.1 = (f32[2048,4096]{1,0:T(8,128)S(1)}, bf16[2048,384]{1,0:T(8,128)(2,1)S(1)}, bf16[384,4096]{1,0:T(8,128)(2,1)S(1)}) custom-call(f32[2048,4096]{1,0:T(8,128)} %refs_0_.1), custom_call_target="tpu_custom_call" | custom-call | tf_op jit(solution)/shard_map/front/pallas_call | solution.py:614
  59.6 12.2 %final.1 = f32[2048,4096]{1,0:T(8,128)} custom-call(f32[2048,4096]{1,0:T(8,128)S(1)} %get-tuple-element.8.refs_0_, bf16[2048,384]{1,0:T(8,128)(2,1)S(1)} %get-tuple-element.9.refs_1_, bf16[384,4096]{1,0:T(8,128)(2,1)S(1)} %get-tuple-element.10.refs_2_), custom_call_target="tpu_custom_call" | custom-call | tf_op jit(solution)/shard_map/final/pallas_call | solution.py:661

commit v4 on v3

--- a/solution.py
+++ b/solution.py
@@ -32,6 +32,11 @@
 def split(x):
     upper = x.astype(bf16)
     return upper, (x - upper.astype(f32)).astype(bf16)
+
+
+def product_halves(left, right):
+    upper, lower = split(right)
+    return jnp.dot(left, jnp.concatenate([upper, upper, lower], axis=0), preferred_element_type=f32)
 
 
 def eliminate(work, rows):
@@ -120,10 +125,10 @@
 
 
 def front_kernel(
-    height, breadth, matrix, block, left, right,
-    slab, strip, pc, pr, halves, own, parts, stats, chained, zs, rs, wr, wc, pe, ps, pt,
+    height, breadth, matrix, block, right, pr, wr, mix,
+    slab, strip, pc, halves, own, parts, stats, chained, zs, near, rs, wc, pe, ps,
     local_sems, block_sems, pc_recvs, ring_sends, mate_sends, pr_recvs, pr_sends, part_sends, part_recvs,
-    stat_sends, stat_recv, chain_send, chain_recv, rs_sends, rs_recvs, wr_right, wr_left, wr_recvs,
+    stat_sends, stat_recv, chain_send, chain_recv, raw_sends, near_recvs, rs_sends, rs_recvs, wr_right, wr_left, wr_recvs,
     role_send, wc_recvs, wc_sends, pe_sends, pe_recvs, pt_sends, pt_recvs,
 ):
     r, c = lax.axis_index("row"), lax.axis_index("col")
@@ -144,6 +149,11 @@
 
     root = r == 0
     edge = c == 0
+    home = r // (height // breadth)
+    low_home = home == 0
+    high_home = home == breadth - 1
+    at_home = jnp.logical_and(high_home, c == breadth - 1)
+    reach = jnp.where(high_home, breadth - 2, breadth - 1)
 
     slab_copy = pltpu.make_async_copy(matrix.at[pl.ds(0, B)], slab, local_sems.at[0])
     strip_copy = pltpu.make_async_copy(matrix.at[:, pl.ds(0, 2 * B)], strip, local_sems.at[1])
@@ -232,9 +242,6 @@
             for part in range(2):
                 ring_copy(i, part, forth).start()
                 ring_copy(half + i, part, back).start()
-        for i in range(height):
-            for part in range(2):
-                mate_copy(i, part).start()
 
     def line_copy(k):
         return remote(pr.at[k], pr.at[k], pr_sends.at[k], pr_recvs.at[k], (r, c + 1))
@@ -247,7 +254,7 @@
         for k in range(breadth - 1, -1, -1):
             line_copy(k).start()
 
-    middle = jnp.logical_and(c >= 1, c < breadth - 1)
+    middle = jnp.logical_and(c >= 1, c < reach)
 
     def line_pass(who, index, when=True):
         k = breadth - 1 - index
@@ -259,9 +266,17 @@
 
     relays = jnp.logical_and(even, jnp.logical_not(root))
 
+    def halve(i):
+        some = slice(i * width, (i + 1) * width)
+        upper, lower = split(pc[i])
+        halves[:B, some] = upper
+        halves[B:, some] = lower
+
     def go_round(pieces):
         for step, (i, part) in enumerate(pieces):
             passed(i, part)
+            if part:
+                halve(i)
             for index in range(breadth):
                 if (index + 1) * len(pieces) // breadth - 1 == step:
                     line_pass(1, index)
@@ -283,6 +298,13 @@
 
     @pl.when(root)
     def _():
+        for i, part in pieces[:height]:
+            ring_copy(i, part, forth).wait_send()
+            ring_copy(half + i, part, back).wait_send()
+        for i, part in pieces:
+            mate_copy(i, part).start()
+        for i in range(height):
+            halve(i)
         for index in range(breadth):
             line_pass(1, index)
 
@@ -316,18 +338,14 @@
             line_pass(1, index)
         for i, part in pieces:
             mate_copy(i, part).wait_recv()
+            if part:
+                halve(i)
 
     @pl.when(even)
     def _():
         for i, part in pieces:
             mate_copy(i, part).wait_send()
         chain_copy.wait_recv()
-
-    @pl.when(root)
-    def _():
-        for i, part in pieces[:height]:
-            ring_copy(i, part, forth).wait_send()
-            ring_copy(half + i, part, back).wait_send()
 
     @pl.when(relays)
     def _():
@@ -345,30 +363,53 @@
     @pl.when(edge)
     def _():
         lower_top(pc)
-
-    for i in range(height):
-        part = slice(i * width, (i + 1) * width)
-        upper, lower = split(pc[i])
-        halves[:B, part] = upper
-        halves[B:, part] = lower
+        for i in range(height):
+            if max(B, i * width) < min(2 * B, (i + 1) * width):
+                halve(i)
+
+    @pl.when(at_home)
+    def _():
+        for k in range(breadth):
+            pr[k] = pc[lax.rem(r * breadth + k, height)]
+
     for copy in block_copies:
         copy.wait()
 
     size = min(512, cols)
 
-    def rs_copy(step, other):
-        return remote(zs.at[other], rs.at[c], rs_sends.at[step], rs_recvs.at[c], (r, other))
-
-    order = sorted(range(1, breadth), key=lambda s: -min(s, breadth - s)) + [0]
-    for index, step in enumerate(order):
-        for k in range(breadth):
-            early = max(0, k - breadth // 4)
-            late = min(breadth - 1, breadth - 2 + k // 2)
-            if 4 * early // breadth == index:
-                line_pass(2, k, r >= 2)
-            if late == index:
-                line_pass(2, k, r < 2)
-        other = lax.rem(c + step, breadth)
+    pair = c // 2
+    late = lax.rem(c, 2)
+    friend = c + 1 - 2 * late
+    pairs = breadth // 2
+
+    def raw_copy(index, k):
+        return remote(zs.at[k], near.at[k], raw_sends.at[index], near_recvs.at[k], (r, friend))
+
+    def sum_of_pair(index, k):
+        return remote(zs.at[k], rs.at[pair], rs_sends.at[index], rs_recvs.at[pair], (r, k))
+
+    def chunk_at(index):
+        if index < breadth - 2:
+            whose = lax.rem(pair + 1 + index // 2, pairs)
+            above = jnp.where(whose > pair, 1, 0)
+            first = jnp.where(whose > pair, 1 - index % 2, index % 2)
+            return 2 * whose + first, above == late
+        return (friend if index == breadth - 2 else c), None
+
+    def add_pair(index):
+        k, adds = chunk_at(index)
+
+        @pl.when(adds)
+        def _():
+            raw_copy(index, k).wait_recv()
+            zs[k] = zs[k] + near[k]
+            sum_of_pair(index, k).start()
+
+    for index in range(breadth):
+        if index in (0, breadth // 2):
+            for k in range(breadth // 2):
+                line_pass(2, k, (r >= 2) if index == 0 else (r < 2))
+        other, adds = chunk_at(index)
         some = pl.ds(pl.multiple_of(other * width, width), width)
         both = jnp.zeros((width, 2 * B), f32)
         for start in range(0, cols, size):
@@ -379,21 +420,25 @@
             both = both + jnp.where(lax.broadcasted_iota(jnp.int32, both.shape, 1) < B, low, f32(0.0))
         turned = both.T
         value = turned[:B, :] + turned[B:, :]
-        if step:
-            zs[other] = value
-            rs_copy(step, other).start()
-        else:
-            rs[c] = value
+        zs[other] = value
+        if index < breadth - 2:
+            pl.when(jnp.logical_not(adds))(raw_copy(index, other).start)
+        elif index == breadth - 2:
+            raw_copy(index, other).start()
+        if index >= 2:
+            add_pair(index - 2)
+    for k in range(breadth // 2, breadth):
+        line_pass(2, k)
     for who in range(3, breadth - 1):
         for k in range(breadth):
             line_pass(who, k)
 
-    for step in range(1, breadth):
-        other = lax.rem(c + step, breadth)
-        remote(rs.at[other], rs.at[other], rs_sends.at[step], rs_recvs.at[other], (r, other)).wait_recv()
-    total = rs[0]
-    for k in range(1, breadth):
-        total = total + rs[k]
+    raw_copy(0, c).wait_recv()
+    total = zs[c] + near[c]
+    for step in range(1, pairs):
+        other = lax.rem(pair + step, pairs)
+        remote(rs.at[other], rs.at[other], rs_sends.at[0], rs_recvs.at[other], (r, friend)).wait_recv()
+        total = total + rs[other]
     wr[c] = total
 
     def sum_copy(k, part, sends, target):
@@ -406,8 +451,10 @@
     def left_copy(k, part):
         return sum_copy(k, part, wr_left, c - 1)
 
-    has_right = c + 1 < breadth
-    has_left = c >= 1
+    has_right = jnp.logical_and(c + 1 < breadth, jnp.logical_not(jnp.logical_and(high_home, c == breadth - 2)))
+    has_left = jnp.logical_and(c >= 1, jnp.logical_not(jnp.logical_and(low_home, c == 1)))
+    takes_right = jnp.logical_not(jnp.logical_and(low_home, edge))
+    takes_left = jnp.logical_not(jnp.logical_and(high_home, c == breadth - 1))
     to_row = lax.rem(me, height)
     to_col = me // height
     itself = jnp.logical_and(to_row == r, to_col == c)
@@ -421,9 +468,9 @@
     def _():
         wc[r] = total
 
-    @pl.when(c == breadth - 1)
-    def _():
-        line_received(breadth - 1)
+    @pl.when(c == reach)
+    def _():
+        line_received(c)
 
     slots = lax.broadcasted_iota(jnp.int32, (B, width), 0)
     positions = lax.broadcasted_iota(jnp.int32, (B, width), 1) + me * width - B
@@ -441,12 +488,12 @@
     def wr_pass(s):
         for part in range(2):
 
-            @pl.when(c - s >= 0)
+            @pl.when(jnp.logical_and(c - s >= 0, takes_left))
             def _():
                 sum_copy(c - s, part, wr_right, c - 1).wait_recv()
                 pl.when(has_right)(right_copy(c - s, part).start)
 
-            @pl.when(c + s < breadth)
+            @pl.when(jnp.logical_and(c + s < breadth, takes_right))
             def _():
                 sum_copy(c + s, part, wr_left, c + 1).wait_recv()
                 pl.when(has_left)(left_copy(c + s, part).start)
@@ -492,25 +539,26 @@
     factor = chained[:, :B]
     turned = factor.T
     inner = product(turned, product(projected[:, :B], factor))
-    mix = jnp.concatenate([turned, -0.5 * inner], axis=1)
+    upper, lower = split(jnp.concatenate([turned, -0.5 * inner], axis=1))
+    mix[...] = jnp.concatenate([upper, lower, upper], axis=1)
     wc_received(mate)
     for step in range(2, height, 2):
         wc_received(lax.rem(mate + step, height))
     for i in range(height):
         part = slice(i * width, (i + 1) * width)
         v = pc[i]
-        u = product(mix, jnp.concatenate([wc[i], v], axis=0))
+        u = product_halves(mix[...], jnp.concatenate([wc[i], v], axis=0))
         upper, lower = split(jnp.concatenate([u, v], axis=0))
         right[: 2 * B, part] = upper
         right[2 * B : 4 * B, part] = upper
         right[4 * B :, part] = lower
 
-    @pl.when(c == breadth - 1)
-    def _():
-        for k in range(breadth - 1):
-            line_received(k)
-
-    @pl.when(c < breadth - 1)
+    @pl.when(c == reach)
+    def _():
+        for k in range(breadth):
+            pl.when(k != c)(lambda: line_received(k))
+
+    @pl.when(c < reach)
     def _():
         for k in range(breadth):
             line_copy(k).wait_send()
@@ -519,14 +567,21 @@
     def _():
         lower_top(pr)
 
-    for i in range(breadth):
-        part = slice(i * width, (i + 1) * width)
-        v = pr[i]
-        u = product(mix, jnp.concatenate([wr[i], v], axis=0))
-        upper, lower = split(jnp.concatenate([v, u], axis=0).T)
-        left[part, : 2 * B] = upper
-        left[part, 2 * B : 4 * B] = lower
-        left[part, 4 * B :] = upper
+    @pl.when(jnp.logical_not(jnp.logical_and(takes_left, takes_right)))
+    def _():
+        for k in range(breadth):
+
+            @pl.when(k != c)
+            def _():
+                wr[k] = wc[lax.rem(r * breadth + k, height)]
+
+    for index in range(breadth - 1):
+        k, adds = chunk_at(index)
+        if adds is None:
+            raw_copy(index, k).wait_send()
+        else:
+            pl.when(adds)(sum_of_pair(index, k).wait_send)
+            pl.when(jnp.logical_not(adds))(raw_copy(index, k).wait_send)
 
     @pl.when(root)
     def _():
@@ -540,7 +595,6 @@
 
     pl.when(odd)(chain_copy.wait_send)
     for step in range(1, breadth):
-        rs_copy(step, lax.rem(c + step, breadth)).wait_send()
         ps_copy(step)[0].wait_send()
     for step in range(1, height):
         pe_copy(step)[0].wait_send()
@@ -572,7 +626,6 @@
         pltpu.VMEM((B, cols), f32),
         pltpu.VMEM((rows, 2 * B), f32),
         pltpu.VMEM((height, B, width), f32),
-        pltpu.VMEM((breadth, B, width), f32),
         pltpu.VMEM((2 * B, cols), bf16),
         pltpu.VMEM((B, 2 * B), f32),
         pltpu.VMEM((breadth, B, 2 * B), f32),
@@ -580,11 +633,10 @@
         pltpu.VMEM((B, 2 * B), f32),
         pltpu.VMEM((breadth, B, width), f32),
         pltpu.VMEM((breadth, B, width), f32),
-        pltpu.VMEM((breadth, B, width), f32),
+        pltpu.VMEM((breadth // 2, B, width), f32),
         pltpu.VMEM((height, B, width), f32),
         pltpu.VMEM((height, B, 2 * B), f32),
         pltpu.VMEM((breadth, B, 2 * B), f32),
-        pltpu.VMEM((B, 2 * B), f32),
         dma((2,)),
         dma((breadth,)),
         dma((height, 2)),
@@ -600,6 +652,8 @@
         dma(()),
         dma((breadth,)),
         dma((breadth,)),
+        dma((breadth,)),
+        dma((breadth // 2,)),
         dma((breadth, 2)),
         dma((breadth, 2)),
         dma((breadth, 2)),
@@ -615,11 +669,13 @@
         lambda *refs: front_kernel(height, breadth, *refs),
         out_shape=[
             pltpu.VMEM((rows, cols), f32),
-            pltpu.VMEM((rows, 6 * B), bf16),
             pltpu.VMEM((6 * B, cols), bf16),
+            pltpu.VMEM((breadth, B, width), f32),
+            pltpu.VMEM((breadth, B, width), f32),
+            pltpu.VMEM((B, 6 * B), bf16),
         ],
         in_specs=[pl.BlockSpec(memory_space=pl.ANY)],
-        out_specs=[vmem] * 3,
+        out_specs=[vmem] * 5,
         scratch_shapes=scratch,
         compiler_params=pltpu.CompilerParams(
             collective_id=0, has_side_effects=True, vmem_limit_bytes=20 << 20
@@ -628,8 +684,9 @@
     )(matrix)
 
 
-def final_kernel(tile, slots, block, left, right, out, buffer, sems):
+def final_kernel(tile, slots, block, right, vr, wr, mix, out, buffer, sems, first_sems):
     rows, cols = block.shape
+    width = vr.shape[2]
     size = min(512, cols)
     count = rows // tile
 
@@ -638,34 +695,56 @@
             buffer.at[i % slots], out.at[pl.ds(i * tile, tile)], sems.at[i % slots]
         )
 
+    def first_copy(at):
+        part = pl.ds(at, size)
+        return pltpu.make_async_copy(
+            buffer.at[0, :, part], out.at[pl.ds(0, tile), part], first_sems.at[at // size]
+        )
+
+    def done(i):
+        if i:
+            copy(i).wait()
+        else:
+            for at in range(0, cols, size):
+                first_copy(at).wait()
+
     for i in range(count):
         if i >= slots:
-            copy(i - slots).wait()
+            done(i - slots)
+        k, at = i * tile // width, i * tile % width
+        v = vr[k, :, at : at + tile]
+        u = product_halves(mix[...], jnp.concatenate([wr[k, :, at : at + tile], v], axis=0))
+        upper, lower = split(jnp.concatenate([v, u], axis=0).T)
+        left = jnp.concatenate([upper, lower, upper], axis=1)
         some = slice(i * tile, (i + 1) * tile)
-        for start in range(0, cols, size):
-            part = slice(start, start + size)
+        for at in range(0, cols, size):
+            part = slice(at, at + size)
             buffer[i % slots, :, part] = block[some, part] - jnp.dot(
-                left[some, :], right[:, part], preferred_element_type=f32
+                left, right[:, part], preferred_element_type=f32
             )
-        copy(i).start()
+            if not i:
+                first_copy(at).start()
+        if i:
+            copy(i).start()
     for i in range(max(0, count - slots), count):
-        copy(i).wait()
-
-
-def final(block, left, right):
+        done(i)
+
+
+def final(block, right, vr, wr, mix):
     rows, cols = block.shape
-    tile = min(256, rows)
+    tile = min(256, vr.shape[2])
     slots = min(4, rows // tile)
     vmem = pl.BlockSpec(memory_space=pltpu.VMEM)
-    held = [pltpu.with_memory_space_constraint(x, pltpu.VMEM) for x in (block, left, right)]
+    held = [pltpu.with_memory_space_constraint(x, pltpu.VMEM) for x in (block, right, vr, wr, mix)]
     return pl.pallas_call(
         lambda *refs: final_kernel(tile, slots, *refs),
         out_shape=jax.ShapeDtypeStruct((rows, cols), f32),
-        in_specs=[vmem] * 3,
+        in_specs=[vmem] * 5,
         out_specs=pl.BlockSpec(memory_space=pl.ANY),
         scratch_shapes=[
             pltpu.VMEM((slots, tile, cols), f32),
             pltpu.SemaphoreType.DMA((slots,)),
+            pltpu.SemaphoreType.DMA((cols // min(512, cols),)),
         ],
         compiler_params=pltpu.CompilerParams(vmem_limit_bytes=20 << 20),
         name="final",

time: 72.6 us -> 71.5 us (0.985)
    pallas_call x1, Pallas kernels: 59.6 us -> 57.9 us  [front(): pl.pallas_call(lambda *refs: front_kernel(height, breadth, *refs), out_sh...]
    pallas_call x1, Pallas kernels: 12.2 us -> 13.3 us  [final(): pl.pallas_call(lambda *refs: final_kernel(tile, slots, *refs), out_shape=...]
where the time goes in v4:
time: 71.5 us; the launch traced here: 71.4 us
  Pallas kernels  71.2 us (100%)
    pallas_call x1, Pallas kernels, front(): pl.pallas_call(lambda *refs: front_kernel(height, breadth, *refs), out_sh...  57.9 us
    pallas_call x1, Pallas kernels, final(): pl.pallas_call(lambda *refs: final_kernel(tile, slots, *refs), out_shape=...  13.3 us

profile of v4, /device:TPU:4, one launch (start us, length us, event | category | flops | bytes accessed | tf_op | source)
XLA Modules:
  0.0 71.4 jit_solution(4673767164193890177)
XLA Ops:
  0.0 57.9 %front.1 = (f32[2048,4096]{1,0:T(8,128)S(1)}, bf16[384,4096]{1,0:T(8,128)(2,1)S(1)}, f32[4,64,512]{2,1,0:T(8,128)S(1)}, f32[4,64,512]{2,1,0:T(8,128)S(1)}, bf16[64,384]{1,0:T(8,128)(2,1)S(1)}) custom-call(f32[2048,4096]{1,0:T(8,128)} %refs_0_.1), custom_call_target="tpu_custom_call" | custom-call | tf_op jit(solution)/shard_map/front/pallas_call | solution.py:668
  57.9 13.3 %final.1 = f32[2048,4096]{1,0:T(8,128)} custom-call(f32[2048,4096]{1,0:T(8,128)S(1)} %get-tuple-element.10.refs_0_, bf16[384,4096]{1,0:T(8,128)(2,1)S(1)} %get-tuple-element.11.refs_1_, f32[4,64,512]{2,1,0:T(8,128)S(1)} %get-tuple-element.12.refs_2_, f32[4,64,512]{2,1,0:T(8,128)S(1)} %get-tuple-element.13.refs_3_, bf16[64,384]{1,0:T(8,128)(2,1)S(1)} %get-tuple-element.14.refs_4_), custom_call_target="tpu_custom_call" | custom-call | tf_op jit(solution)/shard_map/final/pallas_call | solution.py:739

commit v5 on v4

--- a/solution.py
+++ b/solution.py
@@ -7,6 +7,7 @@
 
 B = 64
 STEP = 8
+PIECES = 4
 
 
 highest = lax.Precision.HIGHEST
@@ -125,9 +126,9 @@
 
 
 def front_kernel(
-    height, breadth, matrix, block, right, pr, wr, mix,
-    slab, strip, pc, halves, own, parts, stats, chained, zs, near, rs, wc, pe, ps,
-    local_sems, block_sems, pc_recvs, ring_sends, mate_sends, pr_recvs, pr_sends, part_sends, part_recvs,
+    height, breadth, matrix, block, left, right,
+    slab, strip, pc, pr, wr, halves, own, parts, stats, chained, zs, near, rs, wc, pe, ps,
+    local_sems, block_sems, pc_recvs, ring_far, ring_sends, mate_send, pr_recvs, pr_sends, part_sends, part_recvs,
     stat_sends, stat_recv, chain_send, chain_recv, raw_sends, near_recvs, rs_sends, rs_recvs, wr_right, wr_left, wr_recvs,
     role_send, wc_recvs, wc_sends, pe_sends, pe_recvs, pt_sends, pt_recvs,
 ):
@@ -205,29 +206,38 @@
 
     pl.semaphore_wait(barrier, count - 1)
 
-    def piece_copy(i, part, sends, target):
-        some = pc.at[i, pl.ds(part * (B // 2), B // 2)]
-        return remote(some, some, sends.at[i, part], pc_recvs.at[i, part], (target, c))
+    def piece_copy(i, part, send, target):
+        some = pc.at[i, pl.ds(part * (B // PIECES), B // PIECES)]
+        return remote(some, some, send, pc_recvs.at[i, part], (target, c))
 
     def ring_copy(i, part, target):
-        return piece_copy(i, part, ring_sends, target)
+        return piece_copy(i, part, ring_sends.at[i], target)
 
     def mate_copy(i, part):
-        return piece_copy(i, part, mate_sends, mate)
+        return piece_copy(i, part, mate_send, mate)
+
+    def chunk_sent(i, send):
+        remote(pc.at[i], pc.at[i], send, pc_recvs.at[i, 0], (mate, c)).wait_send()
+
+    def all_sent(send):
+        remote(pc, pc, send, pc_recvs.at[0, 0], (mate, c)).wait_send()
 
     def part_copy(k):
         return remote(own, parts.at[c], part_sends.at[k], part_recvs.at[c], (1, k))
 
     forth = seat(lax.rem(place + 1, half))
     back = seat(lax.rem(place + half - 1, half))
-    goes_forth = place + 1 < half
-    goes_back = place != 1
+    straight = half > 2
+
+    def goes(i):
+        short = 1 if straight and i % half == half - 1 else 0
+        return place + 1 < half - short if i < half else place > 1 + short
+
+    def straight_copy(i, part):
+        return piece_copy(i, part, ring_far.at[i // half], back if i < half else forth)
 
     def ring_on(i, part):
-        if i < half:
-            pl.when(goes_forth)(ring_copy(i, part, forth).start)
-        else:
-            pl.when(goes_back)(ring_copy(i, part, back).start)
+        pl.when(goes(i))(ring_copy(i, part, forth if i < half else back).start)
 
     def passed(i, part):
         mate_copy(i, part).wait_recv()
@@ -239,9 +249,12 @@
         for k in range(breadth):
             part_copy(k).start()
         for i in range(half):
-            for part in range(2):
+            for part in range(PIECES):
                 ring_copy(i, part, forth).start()
                 ring_copy(half + i, part, back).start()
+        for part in range(PIECES if straight else 0):
+            straight_copy(half - 1, part).start()
+            straight_copy(height - 1, part).start()
 
     def line_copy(k):
         return remote(pr.at[k], pr.at[k], pr_sends.at[k], pr_recvs.at[k], (r, c + 1))
@@ -275,14 +288,15 @@
     def go_round(pieces):
         for step, (i, part) in enumerate(pieces):
             passed(i, part)
-            if part:
+            if part == PIECES - 1:
                 halve(i)
             for index in range(breadth):
                 if (index + 1) * len(pieces) // breadth - 1 == step:
                     line_pass(1, index)
 
-    pieces = [(i, part) for i in range(height) for part in range(2)]
-    later = pieces[height:] + pieces[:height]
+    pieces = [(i, part) for i in range(height) for part in range(PIECES)]
+    turn = len(pieces) // 2
+    later = pieces[turn:] + pieces[:turn]
 
     @pl.when(jnp.logical_and(relays, 2 * place < half))
     def _():
@@ -290,7 +304,7 @@
 
     @pl.when(jnp.logical_and(relays, 2 * place == half))
     def _():
-        go_round([piece for pair in zip(pieces[:height], later[:height]) for piece in pair])
+        go_round([piece for pair in zip(pieces[:turn], later[:turn]) for piece in pair])
 
     @pl.when(jnp.logical_and(relays, 2 * place > half))
     def _():
@@ -298,9 +312,11 @@
 
     @pl.when(root)
     def _():
-        for i, part in pieces[:height]:
-            ring_copy(i, part, forth).wait_send()
-            ring_copy(half + i, part, back).wait_send()
+        for i in range(height):
+            chunk_sent(i, ring_sends.at[i])
+        if straight:
+            chunk_sent(half - 1, ring_far.at[0])
+            chunk_sent(height - 1, ring_far.at[1])
         for i, part in pieces:
             mate_copy(i, part).start()
         for i in range(height):
@@ -338,20 +354,18 @@
             line_pass(1, index)
         for i, part in pieces:
             mate_copy(i, part).wait_recv()
-            if part:
+            if part == PIECES - 1:
                 halve(i)
 
     @pl.when(even)
     def _():
-        for i, part in pieces:
-            mate_copy(i, part).wait_send()
+        all_sent(mate_send)
         chain_copy.wait_recv()
 
     @pl.when(relays)
     def _():
-        for i, part in pieces[:height]:
-            pl.when(goes_forth)(ring_copy(i, part, forth).wait_send)
-            pl.when(goes_back)(ring_copy(half + i, part, back).wait_send)
+        for i in range(height):
+            pl.when(goes(i))(lambda: chunk_sent(i, ring_sends.at[i]))
 
     def lower_top(buffer):
         for i in range(buffer.shape[0]):
@@ -540,14 +554,14 @@
     turned = factor.T
     inner = product(turned, product(projected[:, :B], factor))
     upper, lower = split(jnp.concatenate([turned, -0.5 * inner], axis=1))
-    mix[...] = jnp.concatenate([upper, lower, upper], axis=1)
+    mix = jnp.concatenate([upper, lower, upper], axis=1)
     wc_received(mate)
     for step in range(2, height, 2):
         wc_received(lax.rem(mate + step, height))
     for i in range(height):
         part = slice(i * width, (i + 1) * width)
         v = pc[i]
-        u = product_halves(mix[...], jnp.concatenate([wc[i], v], axis=0))
+        u = product_halves(mix, jnp.concatenate([wc[i], v], axis=0))
         upper, lower = split(jnp.concatenate([u, v], axis=0))
         right[: 2 * B, part] = upper
         right[2 * B : 4 * B, part] = upper
@@ -575,6 +589,14 @@
             def _():
                 wr[k] = wc[lax.rem(r * breadth + k, height)]
 
+    for i in range(breadth):
+        part = slice(i * width, (i + 1) * width)
+        v = pr[i]
+        u = product_halves(mix, jnp.concatenate([wr[i], v], axis=0))
+        upper, lower = split(jnp.concatenate([v, u], axis=0).T)
+        left[part, : 2 * B] = upper
+        left[part, 2 * B : 4 * B] = lower
+        left[part, 4 * B :] = upper
     for index in range(breadth - 1):
         k, adds = chunk_at(index)
         if adds is None:
@@ -626,6 +648,8 @@
         pltpu.VMEM((B, cols), f32),
         pltpu.VMEM((rows, 2 * B), f32),
         pltpu.VMEM((height, B, width), f32),
+        pltpu.VMEM((breadth, B, width), f32),
+        pltpu.VMEM((breadth, B, width), f32),
         pltpu.VMEM((2 * B, cols), bf16),
         pltpu.VMEM((B, 2 * B), f32),
         pltpu.VMEM((breadth, B, 2 * B), f32),
@@ -639,9 +663,10 @@
         pltpu.VMEM((breadth, B, 2 * B), f32),
         dma((2,)),
         dma((breadth,)),
-        dma((height, 2)),
-        dma((height, 2)),
-        dma((height, 2)),
+        dma((height, PIECES)),
+        dma((2,)),
+        dma((height,)),
+        dma(()),
         dma((breadth,)),
         dma((breadth,)),
         dma((breadth,)),
@@ -669,13 +694,11 @@
         lambda *refs: front_kernel(height, breadth, *refs),
         out_shape=[
             pltpu.VMEM((rows, cols), f32),
+            pltpu.VMEM((rows, 6 * B), bf16),
             pltpu.VMEM((6 * B, cols), bf16),
-            pltpu.VMEM((breadth, B, width), f32),
-            pltpu.VMEM((breadth, B, width), f32),
-            pltpu.VMEM((B, 6 * B), bf16),
         ],
         in_specs=[pl.BlockSpec(memory_space=pl.ANY)],
-        out_specs=[vmem] * 5,
+        out_specs=[vmem] * 3,
         scratch_shapes=scratch,
         compiler_params=pltpu.CompilerParams(
             collective_id=0, has_side_effects=True, vmem_limit_bytes=20 << 20
@@ -684,9 +707,8 @@
     )(matrix)
 
 
-def final_kernel(tile, slots, block, right, vr, wr, mix, out, buffer, sems, first_sems):
+def final_kernel(tile, slots, block, left, right, out, buffer, sems, first_sems):
     rows, cols = block.shape
-    width = vr.shape[2]
     size = min(512, cols)
     count = rows // tile
 
@@ -711,16 +733,11 @@
     for i in range(count):
         if i >= slots:
             done(i - slots)
-        k, at = i * tile // width, i * tile % width
-        v = vr[k, :, at : at + tile]
-        u = product_halves(mix[...], jnp.concatenate([wr[k, :, at : at + tile], v], axis=0))
-        upper, lower = split(jnp.concatenate([v, u], axis=0).T)
-        left = jnp.concatenate([upper, lower, upper], axis=1)
         some = slice(i * tile, (i + 1) * tile)
         for at in range(0, cols, size):
             part = slice(at, at + size)
             buffer[i % slots, :, part] = block[some, part] - jnp.dot(
-                left, right[:, part], preferred_element_type=f32
+                left[some, :], right[:, part], preferred_element_type=f32
             )
             if not i:
                 first_copy(at).start()
@@ -730,16 +747,16 @@
         done(i)
 
 
-def final(block, right, vr, wr, mix):
+def final(block, left, right):
     rows, cols = block.shape
-    tile = min(256, vr.shape[2])
+    tile = min(256, rows)
     slots = min(4, rows // tile)
     vmem = pl.BlockSpec(memory_space=pltpu.VMEM)
-    held = [pltpu.with_memory_space_constraint(x, pltpu.VMEM) for x in (block, right, vr, wr, mix)]
+    held = [pltpu.with_memory_space_constraint(x, pltpu.VMEM) for x in (block, left, right)]
     return pl.pallas_call(
         lambda *refs: final_kernel(tile, slots, *refs),
         out_shape=jax.ShapeDtypeStruct((rows, cols), f32),
-        in_specs=[vmem] * 5,
+        in_specs=[vmem] * 3,
         out_specs=pl.BlockSpec(memory_space=pl.ANY),
         scratch_shapes=[
             pltpu.VMEM((slots, tile, cols), f32),

time: 71.5 us -> 68.7 us (0.961)
  Pallas kernels: 71.2 us -> 68.4 us
    pallas_call x1, Pallas kernels: 57.9 us -> 56.2 us  [front(): pl.pallas_call(lambda *refs: front_kernel(height, breadth, *refs), out_sh...]
    pallas_call x1, Pallas kernels: 13.3 us -> 12.1 us  [final(): pl.pallas_call(lambda *refs: final_kernel(tile, slots, *refs), out_shape=...]
where the time goes in v5:
time: 68.7 us; the launch traced here: 68.5 us
  Pallas kernels  68.4 us (100%)
    pallas_call x1, Pallas kernels, front(): pl.pallas_call(lambda *refs: front_kernel(height, breadth, *refs), out_sh...  56.2 us
    pallas_call x1, Pallas kernels, final(): pl.pallas_call(lambda *refs: final_kernel(tile, slots, *refs), out_shape=...  12.1 us

profile of v5, /device:TPU:4, one launch (start us, length us, event | category | flops | bytes accessed | tf_op | source)
XLA Modules:
  0.0 68.5 jit_solution(12203681799601040598)
XLA Ops:
  0.0 56.2 %front.1 = (f32[2048,4096]{1,0:T(8,128)S(1)}, bf16[2048,384]{1,0:T(8,128)(2,1)S(1)}, bf16[384,4096]{1,0:T(8,128)(2,1)S(1)}) custom-call(f32[2048,4096]{1,0:T(8,128)} %refs_0_.1), custom_call_target="tpu_custom_call" | custom-call | tf_op jit(solution)/shard_map/front/pallas_call | solution.py:693
  56.2 12.1 %final.1 = f32[2048,4096]{1,0:T(8,128)} custom-call(f32[2048,4096]{1,0:T(8,128)S(1)} %get-tuple-element.8.refs_0_, bf16[2048,384]{1,0:T(8,128)(2,1)S(1)} %get-tuple-element.9.refs_1_, bf16[384,4096]{1,0:T(8,128)(2,1)S(1)} %get-tuple-element.10.refs_2_), custom_call_target="tpu_custom_call" | custom-call | tf_op jit(solution)/shard_map/final/pallas_call | solution.py:756

commit v6 on v5

--- a/solution.py
+++ b/solution.py
@@ -127,10 +127,10 @@
 
 def front_kernel(
     height, breadth, matrix, block, left, right,
-    slab, strip, pc, pr, wr, halves, own, parts, stats, chained, zs, near, rs, wc, pe, ps,
-    local_sems, block_sems, pc_recvs, ring_far, ring_sends, mate_send, pr_recvs, pr_sends, part_sends, part_recvs,
+    slab, strip, pc, pr, wr, halves, own, parts, stats, chained, zs, near, rs, wc, pe, ps, sums,
+    local_sems, block_sems, pc_recvs, ring_far, ring_sends, mate_send, pr_recvs, pr_sends, part_send, part_recvs,
     stat_sends, stat_recv, chain_send, chain_recv, raw_sends, near_recvs, rs_sends, rs_recvs, wr_right, wr_left, wr_recvs,
-    role_send, wc_recvs, wc_sends, pe_sends, pe_recvs, pt_sends, pt_recvs,
+    role_send, wc_recvs, wc_send, pe_send, pe_recvs, ps_send, pt_recvs,
 ):
     r, c = lax.axis_index("row"), lax.axis_index("col")
     rows, cols = matrix.shape
@@ -156,15 +156,32 @@
     at_home = jnp.logical_and(high_home, c == breadth - 1)
     reach = jnp.where(high_home, breadth - 2, breadth - 1)
 
+    pair = c // 2
+    late = lax.rem(c, 2)
+    friend = c + 1 - 2 * late
+    pairs = breadth // 2
+
+    def chunk_at(index):
+        if index < breadth - 2:
+            whose = lax.rem(pair + 1 + index // 2, pairs)
+            above = jnp.where(whose > pair, 1, 0)
+            first = jnp.where(whose > pair, 1 - index % 2, index % 2)
+            return 2 * whose + first, above == late
+        return (friend if index == breadth - 2 else c), None
+
     slab_copy = pltpu.make_async_copy(matrix.at[pl.ds(0, B)], slab, local_sems.at[0])
     strip_copy = pltpu.make_async_copy(matrix.at[:, pl.ds(0, 2 * B)], strip, local_sems.at[1])
     pl.when(root)(slab_copy.start)
     pl.when(edge)(strip_copy.start)
-    block_copies = []
-    for k in range(breadth):
-        part = pl.ds(k * width, width)
-        block_copies.append(pltpu.make_async_copy(matrix.at[part], block.at[part], block_sems.at[k]))
-
+    def block_rows(index):
+        k = chunk_at(index)[0]
+        return pl.ds(pl.multiple_of(k * width, width), width)
+
+    def block_copy(index):
+        part = block_rows(index)
+        return pltpu.make_async_copy(matrix.at[part], block.at[part], block_sems.at[index])
+
+    sums[...] = jnp.zeros_like(sums)
     barrier = pltpu.get_barrier_semaphore()
 
     def greet(step, carry):
@@ -188,8 +205,8 @@
             pc[i] = panel[:, i * width : (i + 1) * width]
 
     pl.when(edge)(strip_copy.wait)
-    for copy in block_copies:
-        copy.start()
+    for index in range(breadth):
+        block_copy(index).start()
 
     @pl.when(root)
     def _():
@@ -223,7 +240,7 @@
         remote(pc, pc, send, pc_recvs.at[0, 0], (mate, c)).wait_send()
 
     def part_copy(k):
-        return remote(own, parts.at[c], part_sends.at[k], part_recvs.at[c], (1, k))
+        return remote(own, parts.at[c], part_send, part_recvs.at[c], (1, k))
 
     forth = seat(lax.rem(place + 1, half))
     back = seat(lax.rem(place + half - 1, half))
@@ -279,11 +296,23 @@
 
     relays = jnp.logical_and(even, jnp.logical_not(root))
 
+    def share(some, part):
+        upper, lower = split(block[some, part])
+        both = lax.dot_general(upper, halves[:, part], NT, preferred_element_type=f32)
+        low = lax.dot_general(lower, halves[:, part], NT, preferred_element_type=f32)
+        return both + jnp.where(lax.broadcasted_iota(jnp.int32, both.shape, 1) < B, low, f32(0.0))
+
+    topmost = [i for i in range(height) if max(B, i * width) < min(2 * B, (i + 1) * width)]
+
     def halve(i):
         some = slice(i * width, (i + 1) * width)
         upper, lower = split(pc[i])
         halves[:B, some] = upper
         halves[B:, some] = lower
+        if i not in topmost:
+            sums[...] = sums[...] + share(block_rows(0), some)
+
+    block_copy(0).wait()
 
     def go_round(pieces):
         for step, (i, part) in enumerate(pieces):
@@ -333,7 +362,7 @@
     def _():
         total = None
         for k in range(breadth):
-            remote(parts.at[k], parts.at[k], part_sends.at[k], part_recvs.at[k], (0, c)).wait_recv()
+            remote(parts.at[k], parts.at[k], part_send, part_recvs.at[k], (0, c)).wait_recv()
             total = parts[k] if total is None else total + parts[k]
         stats[...] = total
         for q in range(1, half):
@@ -377,38 +406,24 @@
     @pl.when(edge)
     def _():
         lower_top(pc)
-        for i in range(height):
-            if max(B, i * width) < min(2 * B, (i + 1) * width):
-                halve(i)
+        for i in topmost:
+            halve(i)
 
     @pl.when(at_home)
     def _():
         for k in range(breadth):
             pr[k] = pc[lax.rem(r * breadth + k, height)]
 
-    for copy in block_copies:
-        copy.wait()
+    for index in range(1, breadth):
+        block_copy(index).wait()
 
     size = min(512, cols)
-
-    pair = c // 2
-    late = lax.rem(c, 2)
-    friend = c + 1 - 2 * late
-    pairs = breadth // 2
 
     def raw_copy(index, k):
         return remote(zs.at[k], near.at[k], raw_sends.at[index], near_recvs.at[k], (r, friend))
 
     def sum_of_pair(index, k):
         return remote(zs.at[k], rs.at[pair], rs_sends.at[index], rs_recvs.at[pair], (r, k))
-
-    def chunk_at(index):
-        if index < breadth - 2:
-            whose = lax.rem(pair + 1 + index // 2, pairs)
-            above = jnp.where(whose > pair, 1, 0)
-            first = jnp.where(whose > pair, 1 - index % 2, index % 2)
-            return 2 * whose + first, above == late
-        return (friend if index == breadth - 2 else c), None
 
     def add_pair(index):
         k, adds = chunk_at(index)
@@ -424,14 +439,15 @@
             for k in range(breadth // 2):
                 line_pass(2, k, (r >= 2) if index == 0 else (r < 2))
         other, adds = chunk_at(index)
-        some = pl.ds(pl.multiple_of(other * width, width), width)
-        both = jnp.zeros((width, 2 * B), f32)
-        for start in range(0, cols, size):
-            part = slice(start, start + size)
-            upper, lower = split(block[some, part])
-            both = both + lax.dot_general(upper, halves[:, part], NT, preferred_element_type=f32)
-            low = lax.dot_general(lower, halves[:, part], NT, preferred_element_type=f32)
-            both = both + jnp.where(lax.broadcasted_iota(jnp.int32, both.shape, 1) < B, low, f32(0.0))
+        some = block_rows(index)
+        if index == 0:
+            both = sums[...]
+            for i in topmost:
+                both = both + share(some, slice(i * width, (i + 1) * width))
+        else:
+            both = jnp.zeros((width, 2 * B), f32)
+            for start in range(0, cols, size):
+                both = both + share(some, slice(start, start + size))
         turned = both.T
         value = turned[:B, :] + turned[B:, :]
         zs[other] = value
@@ -457,7 +473,10 @@
 
     def sum_copy(k, part, sends, target):
         some = wr.at[k, pl.ds(part * (B // 2), B // 2)]
-        return remote(some, some, sends.at[k, part], wr_recvs.at[k, part], (r, target))
+        return remote(some, some, sends.at[k], wr_recvs.at[k, part], (r, target))
+
+    def sum_sent(k, sends):
+        remote(wr.at[k], wr.at[k], sends.at[k], wr_recvs.at[k, 0], (r, c)).wait_send()
 
     def right_copy(k, part):
         return sum_copy(k, part, wr_right, c + 1)
@@ -490,11 +509,12 @@
     positions = lax.broadcasted_iota(jnp.int32, (B, width), 1) + me * width - B
     onehot = jnp.where(positions == slots, f32(1.0), f32(0.0))
     vector = pr[c] - product(chained[:, B:], onehot)
-    pe[r] = jnp.concatenate([product_nt(total, vector), jnp.zeros((B, B), f32)], axis=1)
+    part_of = product_nt(total, vector)
+    pe[r] = jnp.concatenate([part_of[: B // 2], part_of[B // 2 :]], axis=1)
 
     def pe_copy(step):
         other = lax.rem(r + step, height)
-        return remote(pe.at[r], pe.at[r], pe_sends.at[step], pe_recvs.at[r], (other, c)), other
+        return remote(pe.at[r], pe.at[r], pe_send, pe_recvs.at[r], (other, c)), other
 
     for step in range(1, height):
         pe_copy(step)[0].start()
@@ -513,10 +533,10 @@
                 pl.when(has_left)(left_copy(c + s, part).start)
 
     def wc_copy(slot, step, other):
-        return remote(wc.at[slot], wc.at[slot], wc_sends.at[step], wc_recvs.at[slot], (other, c))
+        return remote(wc.at[slot], wc.at[slot], wc_send, wc_recvs.at[slot], (other, c))
 
     def wc_received(slot):
-        remote(wc.at[slot], wc.at[slot], wc_sends.at[0], wc_recvs.at[slot], (mate, c)).wait_recv()
+        remote(wc.at[slot], wc.at[slot], wc_send, wc_recvs.at[slot], (mate, c)).wait_recv()
 
     pl.when(jnp.logical_not(itself))(lambda: wc_received(r))
     for step in range(2, height, 2):
@@ -526,13 +546,13 @@
     summed = pe[r]
     for step in range(1, height):
         copy, other = pe_copy(step)
-        remote(pe.at[other], pe.at[other], pe_sends.at[step], pe_recvs.at[other], (other, c)).wait_recv()
+        remote(pe.at[other], pe.at[other], pe_send, pe_recvs.at[other], (other, c)).wait_recv()
         summed = summed + pe[other]
     ps[c] = summed
 
     def ps_copy(step):
         other = lax.rem(c + step, breadth)
-        return remote(ps.at[c], ps.at[c], pt_sends.at[step], pt_recvs.at[c], (r, other)), other
+        return remote(ps.at[c], ps.at[c], ps_send, pt_recvs.at[c], (r, other)), other
 
     for step in range(1, breadth):
         ps_copy(step)[0].start()
@@ -547,12 +567,13 @@
     projected = ps[c]
     for step in range(1, breadth):
         copy, other = ps_copy(step)
-        remote(ps.at[other], ps.at[other], pt_sends.at[step], pt_recvs.at[other], (r, other)).wait_recv()
+        remote(ps.at[other], ps.at[other], ps_send, pt_recvs.at[other], (r, other)).wait_recv()
         projected = projected + ps[other]
 
+    projected = jnp.concatenate([projected[:, :B], projected[:, B:]], axis=0)
     factor = chained[:, :B]
     turned = factor.T
-    inner = product(turned, product(projected[:, :B], factor))
+    inner = product(turned, product(projected, factor))
     upper, lower = split(jnp.concatenate([turned, -0.5 * inner], axis=1))
     mix = jnp.concatenate([upper, lower, upper], axis=1)
     wc_received(mate)
@@ -607,8 +628,7 @@
 
     @pl.when(root)
     def _():
-        for k in range(breadth):
-            part_copy(k).wait_send()
+        remote(parts, parts, part_send, part_recvs.at[0], (1, c)).wait_send()
 
     @pl.when(r == 1)
     def _():
@@ -616,27 +636,23 @@
             stat_copy(q).wait_send()
 
     pl.when(odd)(chain_copy.wait_send)
-    for step in range(1, breadth):
-        ps_copy(step)[0].wait_send()
-    for step in range(1, height):
-        pe_copy(step)[0].wait_send()
+    several = ps.at[pl.ds(0, breadth - 1)]
+    remote(several, several, ps_send, pt_recvs.at[0], (mate, c)).wait_send()
+    several = pe.at[pl.ds(0, height - 1)]
+    remote(several, several, pe_send, pe_recvs.at[0], (mate, c)).wait_send()
     pl.when(jnp.logical_not(itself))(role.wait_send)
-    for step in range(2, height, 2):
-        wc_copy(r, step, lax.rem(r + step, height)).wait_send()
-        wc_copy(lax.rem(r + step, height), step + 1, mate).wait_send()
-    wc_copy(r, 1, mate).wait_send()
+    several = wc.at[pl.ds(0, height - 1)]
+    remote(several, several, wc_send, wc_recvs.at[0], (mate, c)).wait_send()
 
     @pl.when(has_right)
     def _():
         for k in range(breadth):
-            for part in range(2):
-                pl.when(k <= c)(right_copy(k, part).wait_send)
+            pl.when(k <= c)(lambda: sum_sent(k, wr_right))
 
     @pl.when(has_left)
     def _():
         for k in range(breadth):
-            for part in range(2):
-                pl.when(k >= c)(left_copy(k, part).wait_send)
+            pl.when(k >= c)(lambda: sum_sent(k, wr_left))
 
 
 def front(matrix, height, breadth):
@@ -659,8 +675,9 @@
         pltpu.VMEM((breadth, B, width), f32),
         pltpu.VMEM((breadth // 2, B, width), f32),
         pltpu.VMEM((height, B, width), f32),
-        pltpu.VMEM((height, B, 2 * B), f32),
-        pltpu.VMEM((breadth, B, 2 * B), f32),
+        pltpu.VMEM((height, B // 2, 2 * B), f32),
+        pltpu.VMEM((breadth, B // 2, 2 * B), f32),
+        pltpu.VMEM((width, 2 * B), f32),
         dma((2,)),
         dma((breadth,)),
         dma((height, PIECES)),
@@ -669,7 +686,7 @@
         dma(()),
         dma((breadth,)),
         dma((breadth,)),
-        dma((breadth,)),
+        dma(()),
         dma((breadth,)),
         dma((height // 2,)),
         dma(()),
@@ -679,15 +696,15 @@
         dma((breadth,)),
         dma((breadth,)),
         dma((breadth // 2,)),
-        dma((breadth, 2)),
-        dma((breadth, 2)),
+        dma((breadth,)),
+        dma((breadth,)),
         dma((breadth, 2)),
         dma(()),
         dma((height,)),
+        dma(()),
+        dma(()),
         dma((height,)),
-        dma((height,)),
-        dma((height,)),
-        dma((breadth,)),
+        dma(()),
         dma((breadth,)),
     ]
     return pl.pallas_call(

time: 68.7 us -> 66.9 us (0.974)
  Pallas kernels: 68.4 us -> 66.3 us
    pallas_call x1, Pallas kernels: 56.2 us -> 54.2 us  [front(): pl.pallas_call(lambda *refs: front_kernel(height, breadth, *refs), out_sh...]
where the time goes in v6:
time: 66.9 us; the launch traced here: 66.5 us
  Pallas kernels  66.3 us (99%)
    pallas_call x1, Pallas kernels, front(): pl.pallas_call(lambda *refs: front_kernel(height, breadth, *refs), out_sh...  54.2 us
    pallas_call x1, Pallas kernels, final(): pl.pallas_call(lambda *refs: final_kernel(tile, slots, *refs), out_shape=...  12.1 us

profile of v6, /device:TPU:4, one launch (start us, length us, event | category | flops | bytes accessed | tf_op | source)
XLA Modules:
  0.0 66.5 jit_solution(4289481082508655082)
XLA Ops:
  0.0 54.2 %front.1 = (f32[2048,4096]{1,0:T(8,128)S(1)}, bf16[2048,384]{1,0:T(8,128)(2,1)S(1)}, bf16[384,4096]{1,0:T(8,128)(2,1)S(1)}) custom-call(f32[2048,4096]{1,0:T(8,128)} %refs_0_.1), custom_call_target="tpu_custom_call" | custom-call | tf_op jit(solution)/shard_map/front/pallas_call | solution.py:710
  54.2 12.1 %final.1 = f32[2048,4096]{1,0:T(8,128)} custom-call(f32[2048,4096]{1,0:T(8,128)S(1)} %get-tuple-element.8.refs_0_, bf16[2048,384]{1,0:T(8,128)(2,1)S(1)} %get-tuple-element.9.refs_1_, bf16[384,4096]{1,0:T(8,128)(2,1)S(1)} %get-tuple-element.10.refs_2_), custom_call_target="tpu_custom_call" | custom-call | tf_op jit(solution)/shard_map/final/pallas_call | solution.py:773

commit v7 on v6

--- a/solution.py
+++ b/solution.py
@@ -724,28 +724,21 @@
     )(matrix)
 
 
-def final_kernel(tile, slots, block, left, right, out, buffer, sems, first_sems):
+def final_kernel(tile, slots, size, block, left, right, out, buffer, sems):
     rows, cols = block.shape
-    size = min(512, cols)
     count = rows // tile
 
-    def copy(i):
-        return pltpu.make_async_copy(
-            buffer.at[i % slots], out.at[pl.ds(i * tile, tile)], sems.at[i % slots]
-        )
-
-    def first_copy(at):
+    def copy(i, at):
         part = pl.ds(at, size)
         return pltpu.make_async_copy(
-            buffer.at[0, :, part], out.at[pl.ds(0, tile), part], first_sems.at[at // size]
+            buffer.at[i % slots, :, part],
+            out.at[pl.ds(i * tile, tile), part],
+            sems.at[i % slots, at // size],
         )
 
     def done(i):
-        if i:
-            copy(i).wait()
-        else:
-            for at in range(0, cols, size):
-                first_copy(at).wait()
+        for at in range(0, cols, size):
+            copy(i, at).wait()
 
     for i in range(count):
         if i >= slots:
@@ -756,10 +749,7 @@
             buffer[i % slots, :, part] = block[some, part] - jnp.dot(
                 left[some, :], right[:, part], preferred_element_type=f32
             )
-            if not i:
-                first_copy(at).start()
-        if i:
-            copy(i).start()
+            copy(i, at).start()
     for i in range(max(0, count - slots), count):
         done(i)
 
@@ -768,17 +758,17 @@
     rows, cols = block.shape
     tile = min(256, rows)
     slots = min(4, rows // tile)
+    size = min(512, cols)
     vmem = pl.BlockSpec(memory_space=pltpu.VMEM)
     held = [pltpu.with_memory_space_constraint(x, pltpu.VMEM) for x in (block, left, right)]
     return pl.pallas_call(
-        lambda *refs: final_kernel(tile, slots, *refs),
+        lambda *refs: final_kernel(tile, slots, size, *refs),
         out_shape=jax.ShapeDtypeStruct((rows, cols), f32),
         in_specs=[vmem] * 3,
         out_specs=pl.BlockSpec(memory_space=pl.ANY),
         scratch_shapes=[
             pltpu.VMEM((slots, tile, cols), f32),
-            pltpu.SemaphoreType.DMA((slots,)),
-            pltpu.SemaphoreType.DMA((cols // min(512, cols),)),
+            pltpu.SemaphoreType.DMA((slots, cols // size)),
         ],
         compiler_params=pltpu.CompilerParams(vmem_limit_bytes=20 << 20),
         name="final",

time: 66.9 us -> 66.1 us (0.988)
  Pallas kernels: 66.3 us -> 65.6 us
    pallas_call x1, Pallas kernels: 12.1 us -> 11.4 us  [final(): pl.pallas_call(lambda *refs: final_kernel(tile, slots, size, *refs), out_...]
where the time goes in v7:
time: 66.1 us; the launch traced here: 65.8 us
  Pallas kernels  65.6 us (99%)
    pallas_call x1, Pallas kernels, front(): pl.pallas_call(lambda *refs: front_kernel(height, breadth, *refs), out_sh...  54.2 us
    pallas_call x1, Pallas kernels, final(): pl.pallas_call(lambda *refs: final_kernel(tile, slots, size, *refs), out_...  11.4 us

profile of v7, /device:TPU:4, one launch (start us, length us, event | category | flops | bytes accessed | tf_op | source)
XLA Modules:
  0.0 65.8 jit_solution(5950611327460772267)
XLA Ops:
  0.0 54.2 %front.1 = (f32[2048,4096]{1,0:T(8,128)S(1)}, bf16[2048,384]{1,0:T(8,128)(2,1)S(1)}, bf16[384,4096]{1,0:T(8,128)(2,1)S(1)}) custom-call(f32[2048,4096]{1,0:T(8,128)} %refs_0_.1), custom_call_target="tpu_custom_call" | custom-call | tf_op jit(solution)/shard_map/front/pallas_call | solution.py:710
  54.2 11.4 %final.1 = f32[2048,4096]{1,0:T(8,128)} custom-call(f32[2048,4096]{1,0:T(8,128)S(1)} %get-tuple-element.8.refs_0_, bf16[2048,384]{1,0:T(8,128)(2,1)S(1)} %get-tuple-element.9.refs_1_, bf16[384,4096]{1,0:T(8,128)(2,1)S(1)} %get-tuple-element.10.refs_2_), custom_call_target="tpu_custom_call" | custom-call | tf_op jit(solution)/shard_map/final/pallas_call | solution.py:764
